TPU v7x, 32 devices: a whole 2x2x4 slice. The times are simulated.
32 devices in a mesh: cells: 8 (over z, y), orb: 4 (over x, core).
Axes of the slice: x: 2, y: 2, z: 4, core: 2. Of those that a mesh axis runs over, the one named last changes fastest.
Arguments:
- orbitals: bfloat16 [1024, 256, 512], P('cells', 'orb'), may hold values from -6 to 6
- gradient_matrix: bfloat16 [512, 1536], replicated, may hold values from -0.25 to 0.25
- quad_weights: float32 [512], replicated, may hold values from 0.0009765625 to 0.00390625
- cell_scale: float32 [1024], P('cells'), may hold values from 0.5 to 2
- occupations: float32 [256], P('orb'), may hold values from 0 to 2
- support_cell: int32 [1024], P('cells'), may hold values from 0 to 1023, as said below
- support_atom: int32 [1024], P('cells'), may hold values from -1 to 63, as said below
- proj_values: bfloat16 [1024, 16, 512], P('cells'), may hold values from -6 to 6
- proj_coupling: float32 [64, 16], replicated, may hold values from -0.6 to 0.6
Outputs:
- eshelby: float32 [6, 1024], P(None, 'cells')
- forces: float32 [3, 64], P(None, 'cells')
Inputs may be any that keep to these rules, and one draw needn't show every extreme that they name: `support_cell`: row r lies in the slab of cells from (r // 128) * 128 to that plus 128 - 1. `support_atom`: in each aligned block of 128 rows the live rows (atom 0 or more) come first and padding (-1) after; each such block has 32 or more live rows, and some block is all live. Atom a belongs to slab a // 8; a live row of block s names an atom of a slab (s + d) mod (number of slabs) with d from -2 to 2.
All inputs are finite; a program needn't handle non-finite values.
Results may differ from a plain program's by a relative error of at most 0.0048.
Values sent between devices are 32-bit elements; how exact they have to be, the bound alone decides.
No kernel may reach another device: no remote copies, remote signals or barrier semaphores. Data moves between devices by JAX's collectives and lax.ppermute only.
A program may use at most 192 MiB of HBM per device.

v0:
```python
import math

import jax
import jax.numpy as jnp
from jax import lax
from jax.sharding import PartitionSpec as P

NORB = 256
BLOCK = 128
REACH = 2


def from_behind(shard, axis, by):
    length = lax.axis_size(axis)
    return lax.ppermute(shard, axis, [(i, (i + by) % length) for i in range(length)])


def stress_terms(gradient, weighting):
    grad_x = gradient[:, :, 0]
    grad_y = gradient[:, :, 1]
    grad_z = gradient[:, :, 2]
    half_square = 0.5 * (grad_x * grad_x + grad_y * grad_y + grad_z * grad_z)
    parts = [
        half_square - grad_x * grad_x,
        half_square - grad_y * grad_y,
        half_square - grad_z * grad_z,
        -grad_x * grad_y,
        -grad_x * grad_z,
        -grad_y * grad_z,
    ]
    return jnp.stack([jnp.sum(weighting * part, axis=(1, 2)) for part in parts])


def local(
    orbitals,
    gradient_matrix,
    quad_weights,
    cell_scale,
    occupations,
    support_cell,
    support_atom,
    proj_values,
    proj_coupling,
):
    cell_count, orbital_count, node_count = orbitals.shape
    row_count = support_atom.shape[0]
    proj_count = proj_values.shape[1]
    atom_total = proj_coupling.shape[0]
    slab_total = lax.axis_size("cells")
    atom_share = atom_total // slab_total
    window_slabs = 2 * REACH + 1
    window_atoms = window_slabs * atom_share
    slab_index = lax.axis_index("cells")
    block_cells = math.gcd(cell_count, 16)
    weighting = occupations[:, None] * quad_weights[None, :] / NORB

    def cell_block(pieces):
        block_orbitals, block_scales = pieces
        gradient = jnp.dot(
            block_orbitals.reshape(-1, node_count),
            gradient_matrix,
            preferred_element_type=jnp.float32,
        )
        gradient = gradient.reshape(block_cells, orbital_count, 3, node_count)
        local_weight = weighting[None] * (block_scales**2)[:, None, None]
        stored_block = gradient.astype(jnp.bfloat16).reshape(
            block_cells, orbital_count, 3 * node_count
        )
        return (stress_terms(gradient, local_weight), stored_block)

    blocked = (
        orbitals.reshape(cell_count // block_cells, block_cells, orbital_count, node_count),
        cell_scale.reshape(cell_count // block_cells, block_cells),
    )
    stress_blocks, stored_blocks = lax.map(cell_block, blocked)
    stress_part = jnp.transpose(stress_blocks, (1, 0, 2)).reshape(6, cell_count)
    stored = stored_blocks.reshape(cell_count, orbital_count, 3 * node_count)
    eshelby = lax.psum(stress_part, "orb")
    local_cells = support_cell - slab_index * cell_count
    owner_slab = jnp.floor_divide(jnp.maximum(support_atom, 0), atom_share)
    relative = jnp.mod(owner_slab - slab_index + REACH, slab_total)
    window_ids = relative * atom_share + jnp.mod(jnp.maximum(support_atom, 0), atom_share)
    window_ids = jnp.where(support_atom >= 0, window_ids, -1)
    weighted_proj = (quad_weights[None, None, :] * proj_values).astype(jnp.bfloat16)
    window_range = jnp.arange(window_atoms, dtype=jnp.int32)

    def add_block(block_index, totals):
        scale_here = cell_scale[local_cells]
        picked_orbitals = orbitals[local_cells]
        picked_grad = stored[local_cells].reshape(BLOCK, orbital_count, 3, node_count)
        margin = jnp.einsum(
            "rbq,rnq->rbn", weighted_proj, picked_orbitals, preferred_element_type=jnp.float32
        )
        derivative = jnp.einsum(
            "rbq,rniq->ribn", weighted_proj, picked_grad, preferred_element_type=jnp.float32
        )
        derivative = derivative * scale_here[:, None, None, None]
        stacked = jnp.concatenate([margin[:, None], derivative], axis=1)
        onehot = (window_ids[:, None] == window_range[None, :]).astype(jnp.float32)
        return totals + jnp.einsum(
            "rkbn,ra->kbna", stacked, onehot, precision=lax.Precision.HIGHEST
        )

    initial = jnp.zeros((4, proj_count, orbital_count, window_atoms), jnp.float32)
    block_total = row_count // BLOCK
    window_sums = lax.fori_loop(0, block_total, add_block, initial)
    window_split = window_sums.reshape(4, proj_count, orbital_count, window_slabs, atom_share)
    owned = window_split[:, :, :, REACH]
    for offset in range(-REACH, REACH + 1):
        if offset != 0:
            owned = owned + from_behind(window_split[:, :, :, offset + REACH], "cells", offset)
    coupling = lax.dynamic_slice_in_dim(proj_coupling, slab_index * atom_share, atom_share, 0)
    weight_terms = occupations[None, :, None] * jnp.transpose(coupling)[:, None, :]
    force_part = -2.0 * jnp.sum(owned[1:] * (owned[0] * weight_terms)[None], axis=(1, 2))
    forces = lax.psum(force_part, "orb")
    return (eshelby, forces)


def solution(mesh):
    return jax.shard_map(
        local,
        mesh=mesh,
        in_specs=(
            P("cells", "orb", None),
            P(),
            P(),
            P("cells"),
            P("orb"),
            P("cells"),
            P("cells"),
            P("cells", None, None),
            P(),
        ),
        out_specs=(P(None, "cells"), P(None, "cells")),
        check_vma=False,
    )
```

profile of v0, /device:TPU:0, one launch (start us, length us, event | category | flops | bytes accessed | tf_op | source)
XLA Modules:
  0.0 334.1 jit_solution(303489343255626525)
XLA Ops:
  1.5 2.6 copy.33
  5.3 10.0 %gather_fusion = bf16[128,64,512]{2,1,0:T(8,128)(2,1)} fusion(bf16[128,64,512]{2,1,0:T(8,128)(2,1)} %param.11, s32[1024]{0:T(1024)S(1)} %pad_clamp_fusion), kind=kCustom, calls=%fused_computation | custom fusion | bytes 16777728 | tf_op jit(solution)/shard_map/while/body/eval_jaxpr/gather | solution.py:89
  15.4 179.0 %while.4 = (s32[]{:T(128)}, f32[8,6,16]{2,1,0:T(8,128)S(1)}, bf16[8,16,64,1536]{3,2,1,0:T(8,128)(2,1)}, f32[8,16]{1,0:T(8,128)S(1)}, bf16[8,16,64,512]{3,2,1,0:T...) while((s32[]{:T(128)}, f32[8,6,16]{2,1,0:T(8,128)S(1)}, ...), condition=%wide.region_7.8_spmd.clone, body=%wide.region_0.7_spmd.clone.sunk | while | flops 1626406784 | bytes 37498548 | solution.py:75
  15.4 3.6 %fusion.50 = (bf16[16,64,3,512]{3,1,2,0:T(8,128)(2,1)S(1)}, f32[16,64,3,512]{3,1,2,0:T(8,128)S(1)}) fusion(bf16[3,512,512,1]{2,1,0,3:T(8,128)(2,1)} %bitcast.151, bf16[8,16,64,512]{3,2,1,0:T(8,128)(2,1)} %get-tuple-element.233, s32[]{:T(128)S(6)} %copy.63), kind=kOutput, calls=%fused_computation.77.clone.1 | convolution fusion | flops 1612185600 | bytes 12058628 | tf_op jit(solution)/shard_map/while/body/eval_jaxpr/dot_general | solution.py:59
  19.0 3.7 %fusion.52 = (f32[16]{0:T(128)S(1)}, f32[16]{0:T(128)S(1)}, f32[16]{0:T(128)S(1)}, f32[16]{0:T(128)S(1)}, f32[16]{0:T(128)S(1)}, /*index=5*/f32[16]{0:T(128)S(1)}) fusion(f32[16,64,3,512]{3,1,2,0:T(8,128)S(1)} %get-tuple-element.203, f32[16]{0:T(128)S(1)} %fusion.51, f32[64,512]{1,0:T(8,128)S(1)} %multiply_multiply_fusion.8), kind=kLoop, calls=%fused_computation.15.clone.1 | loop fusion | flops 14155680 | bytes 6422976 | tf_op jit(solution)/shard_map/while/body/eval_jaxpr/reduce_sum | solution.py:31
  22.7 4.7 %copy.57 = bf16[16,64,3,512]{3,2,1,0:T(4,128)(2,1)} copy(bf16[16,64,3,512]{3,1,2,0:T(8,128)(2,1)S(1)} %get-tuple-element.210) | data formatting | bytes 6291456 | tf_op jit(solution)/shard_map/while/body/eval_jaxpr/convert_element_type | solution.py:66
  27.4 8.3 %broadcast_in_dim.48 = bf16[1,16,64,1536]{3,2,1,0:T(8,128)(2,1)S(1)} reshape(bf16[16,64,3,512]{3,2,1,0:T(4,128)(2,1)} %copy.57) | data formatting | bytes 6291456 | tf_op jit(solution)/shard_map/while/body/jit(dynamic_update_index_in_dim)/broadcast_in_dim | solution.py:75
  37.7 3.6 %fusion.50 = (bf16[16,64,3,512]{3,1,2,0:T(8,128)(2,1)S(1)}, f32[16,64,3,512]{3,1,2,0:T(8,128)S(1)}) fusion(bf16[3,512,512,1]{2,1,0,3:T(8,128)(2,1)} %bitcast.151, bf16[8,16,64,512]{3,2,1,0:T(8,128)(2,1)} %get-tuple-element.233, s32[]{:T(128)S(6)} %copy.63), kind=kOutput, calls=%fused_computation.77.clone.1 | convolution fusion | flops 1612185600 | bytes 12058628 | tf_op jit(solution)/shard_map/while/body/eval_jaxpr/dot_general | solution.py:59
  41.4 3.7 %fusion.52 = (f32[16]{0:T(128)S(1)}, f32[16]{0:T(128)S(1)}, f32[16]{0:T(128)S(1)}, f32[16]{0:T(128)S(1)}, f32[16]{0:T(128)S(1)}, /*index=5*/f32[16]{0:T(128)S(1)}) fusion(f32[16,64,3,512]{3,1,2,0:T(8,128)S(1)} %get-tuple-element.203, f32[16]{0:T(128)S(1)} %fusion.51, f32[64,512]{1,0:T(8,128)S(1)} %multiply_multiply_fusion.8), kind=kLoop, calls=%fused_computation.15.clone.1 | loop fusion | flops 14155680 | bytes 6422976 | tf_op jit(solution)/shard_map/while/body/eval_jaxpr/reduce_sum | solution.py:31
  45.1 4.7 %copy.57 = bf16[16,64,3,512]{3,2,1,0:T(4,128)(2,1)} copy(bf16[16,64,3,512]{3,1,2,0:T(8,128)(2,1)S(1)} %get-tuple-element.210) | data formatting | bytes 6291456 | tf_op jit(solution)/shard_map/while/body/eval_jaxpr/convert_element_type | solution.py:66
  49.8 8.3 %broadcast_in_dim.48 = bf16[1,16,64,1536]{3,2,1,0:T(8,128)(2,1)S(1)} reshape(bf16[16,64,3,512]{3,2,1,0:T(4,128)(2,1)} %copy.57) | data formatting | bytes 6291456 | tf_op jit(solution)/shard_map/while/body/jit(dynamic_update_index_in_dim)/broadcast_in_dim | solution.py:75
  58.2 2.0 constant_dynamic-update-slice_fusion.2
  60.1 3.6 %fusion.50 = (bf16[16,64,3,512]{3,1,2,0:T(8,128)(2,1)S(1)}, f32[16,64,3,512]{3,1,2,0:T(8,128)S(1)}) fusion(bf16[3,512,512,1]{2,1,0,3:T(8,128)(2,1)} %bitcast.151, bf16[8,16,64,512]{3,2,1,0:T(8,128)(2,1)} %get-tuple-element.233, s32[]{:T(128)S(6)} %copy.63), kind=kOutput, calls=%fused_computation.77.clone.1 | convolution fusion | flops 1612185600 | bytes 12058628 | tf_op jit(solution)/shard_map/while/body/eval_jaxpr/dot_general | solution.py:59
  63.8 3.7 %fusion.52 = (f32[16]{0:T(128)S(1)}, f32[16]{0:T(128)S(1)}, f32[16]{0:T(128)S(1)}, f32[16]{0:T(128)S(1)}, f32[16]{0:T(128)S(1)}, /*index=5*/f32[16]{0:T(128)S(1)}) fusion(f32[16,64,3,512]{3,1,2,0:T(8,128)S(1)} %get-tuple-element.203, f32[16]{0:T(128)S(1)} %fusion.51, f32[64,512]{1,0:T(8,128)S(1)} %multiply_multiply_fusion.8), kind=kLoop, calls=%fused_computation.15.clone.1 | loop fusion | flops 14155680 | bytes 6422976 | tf_op jit(solution)/shard_map/while/body/eval_jaxpr/reduce_sum | solution.py:31
  67.5 4.7 %copy.57 = bf16[16,64,3,512]{3,2,1,0:T(4,128)(2,1)} copy(bf16[16,64,3,512]{3,1,2,0:T(8,128)(2,1)S(1)} %get-tuple-element.210) | data formatting | bytes 6291456 | tf_op jit(solution)/shard_map/while/body/eval_jaxpr/convert_element_type | solution.py:66
  72.2 8.3 %broadcast_in_dim.48 = bf16[1,16,64,1536]{3,2,1,0:T(8,128)(2,1)S(1)} reshape(bf16[16,64,3,512]{3,2,1,0:T(4,128)(2,1)} %copy.57) | data formatting | bytes 6291456 | tf_op jit(solution)/shard_map/while/body/jit(dynamic_update_index_in_dim)/broadcast_in_dim | solution.py:75
  82.5 3.6 %fusion.50 = (bf16[16,64,3,512]{3,1,2,0:T(8,128)(2,1)S(1)}, f32[16,64,3,512]{3,1,2,0:T(8,128)S(1)}) fusion(bf16[3,512,512,1]{2,1,0,3:T(8,128)(2,1)} %bitcast.151, bf16[8,16,64,512]{3,2,1,0:T(8,128)(2,1)} %get-tuple-element.233, s32[]{:T(128)S(6)} %copy.63), kind=kOutput, calls=%fused_computation.77.clone.1 | convolution fusion | flops 1612185600 | bytes 12058628 | tf_op jit(solution)/shard_map/while/body/eval_jaxpr/dot_general | solution.py:59
  86.2 3.7 %fusion.52 = (f32[16]{0:T(128)S(1)}, f32[16]{0:T(128)S(1)}, f32[16]{0:T(128)S(1)}, f32[16]{0:T(128)S(1)}, f32[16]{0:T(128)S(1)}, /*index=5*/f32[16]{0:T(128)S(1)}) fusion(f32[16,64,3,512]{3,1,2,0:T(8,128)S(1)} %get-tuple-element.203, f32[16]{0:T(128)S(1)} %fusion.51, f32[64,512]{1,0:T(8,128)S(1)} %multiply_multiply_fusion.8), kind=kLoop, calls=%fused_computation.15.clone.1 | loop fusion | flops 14155680 | bytes 6422976 | tf_op jit(solution)/shard_map/while/body/eval_jaxpr/reduce_sum | solution.py:31
  89.9 4.7 %copy.57 = bf16[16,64,3,512]{3,2,1,0:T(4,128)(2,1)} copy(bf16[16,64,3,512]{3,1,2,0:T(8,128)(2,1)S(1)} %get-tuple-element.210) | data formatting | bytes 6291456 | tf_op jit(solution)/shard_map/while/body/eval_jaxpr/convert_element_type | solution.py:66
  94.6 8.3 %broadcast_in_dim.48 = bf16[1,16,64,1536]{3,2,1,0:T(8,128)(2,1)S(1)} reshape(bf16[16,64,3,512]{3,2,1,0:T(4,128)(2,1)} %copy.57) | data formatting | bytes 6291456 | tf_op jit(solution)/shard_map/while/body/jit(dynamic_update_index_in_dim)/broadcast_in_dim | solution.py:75
  104.9 3.6 %fusion.50 = (bf16[16,64,3,512]{3,1,2,0:T(8,128)(2,1)S(1)}, f32[16,64,3,512]{3,1,2,0:T(8,128)S(1)}) fusion(bf16[3,512,512,1]{2,1,0,3:T(8,128)(2,1)} %bitcast.151, bf16[8,16,64,512]{3,2,1,0:T(8,128)(2,1)} %get-tuple-element.233, s32[]{:T(128)S(6)} %copy.63), kind=kOutput, calls=%fused_computation.77.clone.1 | convolution fusion | flops 1612185600 | bytes 12058628 | tf_op jit(solution)/shard_map/while/body/eval_jaxpr/dot_general | solution.py:59
  108.5 3.7 %fusion.52 = (f32[16]{0:T(128)S(1)}, f32[16]{0:T(128)S(1)}, f32[16]{0:T(128)S(1)}, f32[16]{0:T(128)S(1)}, f32[16]{0:T(128)S(1)}, /*index=5*/f32[16]{0:T(128)S(1)}) fusion(f32[16,64,3,512]{3,1,2,0:T(8,128)S(1)} %get-tuple-element.203, f32[16]{0:T(128)S(1)} %fusion.51, f32[64,512]{1,0:T(8,128)S(1)} %multiply_multiply_fusion.8), kind=kLoop, calls=%fused_computation.15.clone.1 | loop fusion | flops 14155680 | bytes 6422976 | tf_op jit(solution)/shard_map/while/body/eval_jaxpr/reduce_sum | solution.py:31
  112.2 4.7 %copy.57 = bf16[16,64,3,512]{3,2,1,0:T(4,128)(2,1)} copy(bf16[16,64,3,512]{3,1,2,0:T(8,128)(2,1)S(1)} %get-tuple-element.210) | data formatting | bytes 6291456 | tf_op jit(solution)/shard_map/while/body/eval_jaxpr/convert_element_type | solution.py:66
  116.9 8.3 %broadcast_in_dim.48 = bf16[1,16,64,1536]{3,2,1,0:T(8,128)(2,1)S(1)} reshape(bf16[16,64,3,512]{3,2,1,0:T(4,128)(2,1)} %copy.57) | data formatting | bytes 6291456 | tf_op jit(solution)/shard_map/while/body/jit(dynamic_update_index_in_dim)/broadcast_in_dim | solution.py:75
  127.2 3.6 %fusion.50 = (bf16[16,64,3,512]{3,1,2,0:T(8,128)(2,1)S(1)}, f32[16,64,3,512]{3,1,2,0:T(8,128)S(1)}) fusion(bf16[3,512,512,1]{2,1,0,3:T(8,128)(2,1)} %bitcast.151, bf16[8,16,64,512]{3,2,1,0:T(8,128)(2,1)} %get-tuple-element.233, s32[]{:T(128)S(6)} %copy.63), kind=kOutput, calls=%fused_computation.77.clone.1 | convolution fusion | flops 1612185600 | bytes 12058628 | tf_op jit(solution)/shard_map/while/body/eval_jaxpr/dot_general | solution.py:59
  130.9 3.7 %fusion.52 = (f32[16]{0:T(128)S(1)}, f32[16]{0:T(128)S(1)}, f32[16]{0:T(128)S(1)}, f32[16]{0:T(128)S(1)}, f32[16]{0:T(128)S(1)}, /*index=5*/f32[16]{0:T(128)S(1)}) fusion(f32[16,64,3,512]{3,1,2,0:T(8,128)S(1)} %get-tuple-element.203, f32[16]{0:T(128)S(1)} %fusion.51, f32[64,512]{1,0:T(8,128)S(1)} %multiply_multiply_fusion.8), kind=kLoop, calls=%fused_computation.15.clone.1 | loop fusion | flops 14155680 | bytes 6422976 | tf_op jit(solution)/shard_map/while/body/eval_jaxpr/reduce_sum | solution.py:31
  134.6 4.7 %copy.57 = bf16[16,64,3,512]{3,2,1,0:T(4,128)(2,1)} copy(bf16[16,64,3,512]{3,1,2,0:T(8,128)(2,1)S(1)} %get-tuple-element.210) | data formatting | bytes 6291456 | tf_op jit(solution)/shard_map/while/body/eval_jaxpr/convert_element_type | solution.py:66
  139.3 8.3 %broadcast_in_dim.48 = bf16[1,16,64,1536]{3,2,1,0:T(8,128)(2,1)S(1)} reshape(bf16[16,64,3,512]{3,2,1,0:T(4,128)(2,1)} %copy.57) | data formatting | bytes 6291456 | tf_op jit(solution)/shard_map/while/body/jit(dynamic_update_index_in_dim)/broadcast_in_dim | solution.py:75
  149.6 3.6 %fusion.50 = (bf16[16,64,3,512]{3,1,2,0:T(8,128)(2,1)S(1)}, f32[16,64,3,512]{3,1,2,0:T(8,128)S(1)}) fusion(bf16[3,512,512,1]{2,1,0,3:T(8,128)(2,1)} %bitcast.151, bf16[8,16,64,512]{3,2,1,0:T(8,128)(2,1)} %get-tuple-element.233, s32[]{:T(128)S(6)} %copy.63), kind=kOutput, calls=%fused_computation.77.clone.1 | convolution fusion | flops 1612185600 | bytes 12058628 | tf_op jit(solution)/shard_map/while/body/eval_jaxpr/dot_general | solution.py:59
  153.3 3.7 %fusion.52 = (f32[16]{0:T(128)S(1)}, f32[16]{0:T(128)S(1)}, f32[16]{0:T(128)S(1)}, f32[16]{0:T(128)S(1)}, f32[16]{0:T(128)S(1)}, /*index=5*/f32[16]{0:T(128)S(1)}) fusion(f32[16,64,3,512]{3,1,2,0:T(8,128)S(1)} %get-tuple-element.203, f32[16]{0:T(128)S(1)} %fusion.51, f32[64,512]{1,0:T(8,128)S(1)} %multiply_multiply_fusion.8), kind=kLoop, calls=%fused_computation.15.clone.1 | loop fusion | flops 14155680 | bytes 6422976 | tf_op jit(solution)/shard_map/while/body/eval_jaxpr/reduce_sum | solution.py:31
  157.0 4.7 %copy.57 = bf16[16,64,3,512]{3,2,1,0:T(4,128)(2,1)} copy(bf16[16,64,3,512]{3,1,2,0:T(8,128)(2,1)S(1)} %get-tuple-element.210) | data formatting | bytes 6291456 | tf_op jit(solution)/shard_map/while/body/eval_jaxpr/convert_element_type | solution.py:66
  161.7 8.3 %broadcast_in_dim.48 = bf16[1,16,64,1536]{3,2,1,0:T(8,128)(2,1)S(1)} reshape(bf16[16,64,3,512]{3,2,1,0:T(4,128)(2,1)} %copy.57) | data formatting | bytes 6291456 | tf_op jit(solution)/shard_map/while/body/jit(dynamic_update_index_in_dim)/broadcast_in_dim | solution.py:75
  172.0 3.6 %fusion.50 = (bf16[16,64,3,512]{3,1,2,0:T(8,128)(2,1)S(1)}, f32[16,64,3,512]{3,1,2,0:T(8,128)S(1)}) fusion(bf16[3,512,512,1]{2,1,0,3:T(8,128)(2,1)} %bitcast.151, bf16[8,16,64,512]{3,2,1,0:T(8,128)(2,1)} %get-tuple-element.233, s32[]{:T(128)S(6)} %copy.63), kind=kOutput, calls=%fused_computation.77.clone.1 | convolution fusion | flops 1612185600 | bytes 12058628 | tf_op jit(solution)/shard_map/while/body/eval_jaxpr/dot_general | solution.py:59
  175.6 3.7 %fusion.52 = (f32[16]{0:T(128)S(1)}, f32[16]{0:T(128)S(1)}, f32[16]{0:T(128)S(1)}, f32[16]{0:T(128)S(1)}, f32[16]{0:T(128)S(1)}, /*index=5*/f32[16]{0:T(128)S(1)}) fusion(f32[16,64,3,512]{3,1,2,0:T(8,128)S(1)} %get-tuple-element.203, f32[16]{0:T(128)S(1)} %fusion.51, f32[64,512]{1,0:T(8,128)S(1)} %multiply_multiply_fusion.8), kind=kLoop, calls=%fused_computation.15.clone.1 | loop fusion | flops 14155680 | bytes 6422976 | tf_op jit(solution)/shard_map/while/body/eval_jaxpr/reduce_sum | solution.py:31
  179.3 4.7 %copy.57 = bf16[16,64,3,512]{3,2,1,0:T(4,128)(2,1)} copy(bf16[16,64,3,512]{3,1,2,0:T(8,128)(2,1)S(1)} %get-tuple-element.210) | data formatting | bytes 6291456 | tf_op jit(solution)/shard_map/while/body/eval_jaxpr/convert_element_type | solution.py:66
  184.0 8.3 %broadcast_in_dim.48 = bf16[1,16,64,1536]{3,2,1,0:T(8,128)(2,1)S(1)} reshape(bf16[16,64,3,512]{3,2,1,0:T(4,128)(2,1)} %copy.57) | data formatting | bytes 6291456 | tf_op jit(solution)/shard_map/while/body/jit(dynamic_update_index_in_dim)/broadcast_in_dim | solution.py:75
  194.3 19.2 %gather_fusion.1 = bf16[128,64,1536]{2,1,0:T(8,128)(2,1)} fusion(bf16[128,64,1536]{2,1,0:T(8,128)(2,1)} %bitcast.159, s32[1024]{0:T(1024)S(1)} %pad_clamp_fusion), kind=kCustom, calls=%fused_computation.1 | custom fusion | bytes 50332160 | tf_op jit(solution)/shard_map/while/body/eval_jaxpr/gather | solution.py:90
  213.6 34.0 %copy.35 = bf16[128,64,1536]{0,2,1:T(8,128)(2,1)} copy(bf16[128,64,1536]{2,1,0:T(8,128)(2,1)} %gather_fusion.1) | data formatting | bytes 50331648 | tf_op jit(solution)/shard_map/while/body/eval_jaxpr/gather | solution.py:90
  247.5 31.3 %copy.36 = bf16[128,64,3,512]{3,1,2,0:T(8,128)(2,1)} copy(bf16[128,64,3,512]{0,3,2,1:T(8,128)(2,1)} %bitcast.158) | data formatting | bytes 50331648 | tf_op jit(solution)/shard_map/while/body/eval_jaxpr/reshape | solution.py:90
  278.9 6.7 %fusion.28 = f32[128,1,16,64]{3,2,1,0:T(8,128)} fusion(bf16[128,64,512]{2,1,0:T(8,128)(2,1)} %gather_fusion, bf16[128,16,512]{2,1,0:T(8,128)(2,1)S(1)} %copy-done.2, f32[512]{0:T(512)S(1)} %get-tuple-element.246), kind=kOutput, calls=%fused_computation.46 | convolution fusion | flops 137363456 | bytes 11012096 | tf_op jit(solution)/shard_map/while/body/eval_jaxpr/rbq,rnq->rbn/dot_general | solution.py:91
  285.6 12.0 %multiply_bitcast_fusion = f32[128,3,16,64]{3,2,1,0:T(8,128)S(1)} fusion(f32[128]{0:T(128)S(1)} %gather_fusion.2, bf16[128,64,3,512]{3,1,2,0:T(8,128)(2,1)} %copy.36, bf16[128,16,512]{2,1,0:T(8,128)(2,1)} %param.18, f32[512]{0:T(512)S(1)} %get-tuple-element.246), kind=kOutput, calls=%fused_computation.41 | convolution fusion | flops 406192128 | bytes 28838400 | tf_op jit(solution)/shard_map/while/body/eval_jaxpr/rbq,rniq->ribn/dot_general | solution.py:94
  299.5 4.0 %fusion.25 = f32[4,16,64,5,8]{2,4,3,1,0:T(8,128)S(1)} fusion(f32[128,4,16,64]{3,2,1,0:T(8,128)S(1)} %pad_maximum_fusion, s32[128]{0:T(128)S(1)} %compare_select_fusion.3), kind=kOutput, calls=%fused_computation.45 | convolution fusion | flops 251663360 | bytes 2753024 | tf_op jit(solution)/shard_map/while/body/eval_jaxpr/rkbn,ra->kbna/dot_general | solution.py:100
  303.6 3.1 collective-permute-start.3
  308.2 3.2 collective-permute-start.1
  311.9 4.0 %collective-permute-done.3 = f32[4,16,64,8]{2,3,1,0:T(8,128)S(1)} collective-permute-done((f32[4,16,64,8]{2,3,1,0:T(8,128)S(1)}, f32[4,16,64,8]{2,3,1,0:T(8,128)S(1)}, u32[]{:S(2)}, u32[]{:S(2)}) %collective-permute-start.3) | collective-permute-done | bytes 131104 | tf_op jit(solution)/shard_map/ppermute | solution.py:15
  315.9 6.8 %collective-permute-done.2 = f32[4,16,64,8]{2,3,1,0:T(8,128)S(1)} collective-permute-done((f32[4,16,64,8]{2,3,1,0:T(8,128)S(1)}, f32[4,16,64,8]{2,3,1,0:T(8,128)S(1)}, u32[]{:S(2)}, u32[]{:S(2)}) %collective-permute-start.2) | collective-permute-done | bytes 131104 | tf_op jit(solution)/shard_map/ppermute | solution.py:15
  322.7 3.6 %collective-permute-done = f32[4,16,64,8]{2,3,1,0:T(8,128)S(1)} collective-permute-done((f32[4,16,64,8]{2,3,1,0:T(8,128)S(1)}, f32[4,16,64,8]{2,3,1,0:T(8,128)S(1)}, u32[]{:S(2)}, u32[]{:S(2)}) %collective-permute-start) | collective-permute-done | bytes 131104 | tf_op jit(solution)/shard_map/ppermute | solution.py:15
  326.5 7.5 %all-reduce = (f32[6,128]{1,0:T(8,128)}, f32[3,8]{1,0:T(4,128)}) all-reduce(f32[6,128]{1,0:T(8,128)S(1)} %reshape.55, f32[3,8]{1,0:T(4,128)S(1)} %broadcast_multiply_fusion), channel_id=1, replica_groups=mesh['cells'=8,'orb'=4] {'orb'}, use_global_device_ids=true, to_apply=%region_8.9 | all-reduce | flops 792 | bytes 6336 | tf_op jit(solution)/shard_map/psum | solution.py:78
  (72 shorter events, 20.9 us)
Async XLA Ops:
  0.6 311.2 %copy-start = (f32[64,16]{0,1:T(8,128)S(1)}, f32[64,16]{0,1:T(8,128)}, u32[]{:S(2)}) copy-start(f32[64,16]{0,1:T(8,128)} %param.19) | copy-start | bytes 12292
  0.6 3.4 %copy-start.1 = (f32[128]{0:T(128)S(1)}, f32[128]{0:T(128)}, u32[]{:S(2)}) copy-start(f32[128]{0:T(128)} %param.14) | copy-start | bytes 1540
  0.7 3.4 %copy-start.5 = (s32[128]{0:T(128)S(1)}, s32[128]{0:T(128)}, u32[]{:S(2)}) copy-start(s32[128]{0:T(128)} %param.16) | copy-start | bytes 1540
  5.3 10.1 %copy-start.3 = (f32[512]{0:T(512)S(1)}, f32[512]{0:T(512)}, u32[]{:S(2)}) copy-start(f32[512]{0:T(512)} %param.13) | copy-start | bytes 6148
  5.3 10.0 %copy-start.4 = (f32[64]{0:T(128)S(1)}, f32[64]{0:T(128)}, u32[]{:S(2)}) copy-start(f32[64]{0:T(128)} %param.15) | copy-start | bytes 772
  247.5 31.3 %copy-start.6 = (s32[128]{0:T(128)S(1)}, s32[128]{0:T(128)}, u32[]{:S(2)}) copy-start(s32[128]{0:T(128)} %param.17) | copy-start | bytes 1540
  247.5 31.3 %copy-start.2 = (bf16[128,16,512]{2,1,0:T(8,128)(2,1)S(1)}, bf16[128,16,512]{2,1,0:T(8,128)(2,1)}, u32[]{:S(2)}) copy-start(bf16[128,16,512]{2,1,0:T(8,128)(2,1)} %param.18) | copy-start | bytes 6291460
  303.6 12.3 %collective-permute-start.3 = (f32[4,16,64,8]{2,3,1,0:T(8,128)S(1)}, f32[4,16,64,8]{2,3,1,0:T(8,128)S(1)}, u32[]{:S(2)}, u32[]{:S(2)}) collective-permute-start(f32[4,16,64,8]{2,3,1,0:T(8,128)S(1)} %get-tuple-element.144), channel_id=1, source_target_pairs={{0,8},{4,12},{8,16},{12,20},{16,24},{20,28},{24,0},{28,4},{1,9},{5... | collective-permute-start | bytes 393224 | tf_op jit(solution)/shard_map/ppermute | solution.py:15
  306.7 16.0 %collective-permute-start.2 = (f32[4,16,64,8]{2,3,1,0:T(8,128)S(1)}, f32[4,16,64,8]{2,3,1,0:T(8,128)S(1)}, u32[]{:S(2)}, u32[]{:S(2)}) collective-permute-start(f32[4,16,64,8]{2,3,1,0:T(8,128)S(1)} %get-tuple-element.145), channel_id=1, source_target_pairs={{0,4},{4,8},{8,12},{12,16},{16,20},{20,24},{24,28},{28,0},{1,5},{5... | collective-permute-start | bytes 393224 | tf_op jit(solution)/shard_map/ppermute | solution.py:15
  308.2 14.5 %collective-permute-start.1 = (f32[4,16,64,8]{2,3,1,0:T(8,128)S(1)}, f32[4,16,64,8]{2,3,1,0:T(8,128)S(1)}, u32[]{:S(2)}, u32[]{:S(2)}) collective-permute-start(f32[4,16,64,8]{2,3,1,0:T(8,128)S(1)} %get-tuple-element.143), channel_id=1, source_target_pairs={{0,28},{4,0},{8,4},{12,8},{16,12},{20,16},{24,20},{28,24},{1,29},{... | collective-permute-start | bytes 393224 | tf_op jit(solution)/shard_map/ppermute | solution.py:15
  311.4 14.8 %collective-permute-start = (f32[4,16,64,8]{2,3,1,0:T(8,128)S(1)}, f32[4,16,64,8]{2,3,1,0:T(8,128)S(1)}, u32[]{:S(2)}, u32[]{:S(2)}) collective-permute-start(f32[4,16,64,8]{2,3,1,0:T(8,128)S(1)} %get-tuple-element.142), channel_id=1, source_target_pairs={{0,24},{4,28},{8,0},{12,4},{16,8},{20,12},{24,16},{28,20},{1,25},{... | collective-permute-start | bytes 393224 | tf_op jit(solution)/shard_map/ppermute | solution.py:15
where the time goes:
time: 337 us; the launch traced here: 334 us
  local copies, waits for them, and re-layouts  220 us (65%)
  matrix products  51.2 us (15%)
  other arithmetic  32.1 us (10%)
  waiting for transfers between devices  14.4 us (4%)
  starting transfers between devices  8.11 us (2%)
  blocking collectives  7.53 us (2%)
    broadcast_in_dim x8, local copies, waits for them, and re-layouts, local(): stress_blocks, stored_blocks = lax.map(cell_block, blocked)  66.7 us
    gather x2, local copies, waits for them, and re-layouts, add_block(): stored[local_cells].reshape(BLOCK, orbital_count, 3, node_count)  53.2 us
    convert_element_type x8, local copies, waits for them, and re-layouts, cell_block(): gradient.astype(jnp.bfloat16)  37.6 us
    reshape x1, local copies, waits for them, and re-layouts, add_block(): stored[local_cells].reshape(BLOCK, orbital_count, 3, node_count)  31.3 us
    reduce_sum x8, other arithmetic, stress_terms(): return jnp.stack([jnp.sum(weighting * part, axis=(1, 2)) for part in parts])  29.2 us
    dot_general x8, matrix products, cell_block(): jnp.dot(block_orbitals.reshape(-1, node_count), gradient_matrix, preferre...  28.4 us
    dynamic_update_slice x16, local copies, waits for them, and re-layouts, local(): stress_blocks, stored_blocks = lax.map(cell_block, blocked)  15.8 us
    ppermute x4, waiting for transfers between devices, from_behind(): lax.ppermute(shard, axis, [(i, (i + by) % length) for i in range(length)])  14.4 us
  transfers between devices with their start and end apart: 4, of which 3 were waited for; matrix products, arithmetic and copies ran while one was open for 0% of the time, Pallas kernels for 0%

commit v1 on v0

v1 whole, which is shorter than its diff:
```python
import functools

import jax
import jax.numpy as jnp
from jax import lax
from jax.experimental import pallas as pl
from jax.experimental.pallas import tpu as pltpu
from jax.sharding import PartitionSpec as P

REACH = 2
LANES = 128
PAIRS = ((0, 0), (1, 1), (2, 2), (0, 1), (0, 2), (1, 2))
CONTRACT_LAST = (((1,), (1,)), ((), ()))


def from_behind(shard, axis, by):
    length = lax.axis_size(axis)
    return lax.ppermute(shard, axis, [(i, (i + by) % length) for i in range(length)])


def force_kernel(
    cell_ref,
    window_ref,
    scale_ref,
    weight_ref,
    proj_ref,
    matrix_ref,
    orbitals_hbm,
    *rest,
    window_slabs,
    chunk,
    unroll,
):
    outs = rest[:window_slabs]
    folded, orbitals_ref, acc, sem = rest[window_slabs:]
    rows, parts, projs, nodes = folded.shape
    atoms = outs[0].shape[0]
    orbs = orbitals_ref.shape[1]
    load = pltpu.make_async_copy(orbitals_hbm, orbitals_ref, sem)
    load.start()
    acc[...] = jnp.zeros_like(acc)

    def fold(step, carry):
        at = pl.ds(pl.multiple_of(step * chunk, chunk), chunk)
        scaled = proj_ref[at].astype(jnp.float32) * weight_ref[...][None]
        scaled = scaled.astype(jnp.bfloat16)
        folded[at, 0] = scaled
        flat = scaled.reshape(chunk * projs, nodes)
        for i in range(parts - 1):
            part = lax.dot_general(
                flat,
                matrix_ref[:, i * nodes : (i + 1) * nodes],
                CONTRACT_LAST,
                preferred_element_type=jnp.float32,
            )
            folded[at, i + 1] = part.astype(jnp.bfloat16).reshape(chunk, projs, nodes)
        return carry

    lax.fori_loop(0, rows // chunk, fold, 0)
    load.wait()

    def add_rows(step, carry):
        for j in range(unroll):
            row = step * unroll + j
            cell = cell_ref[row]
            slot = window_ref[row]
            term = lax.dot_general(
                folded[row].reshape(parts * projs, nodes),
                orbitals_ref[cell],
                CONTRACT_LAST,
                preferred_element_type=jnp.float32,
            )
            acc[slot, :projs] += term[:projs]
            acc[slot, projs:] += term[projs:] * scale_ref[cell]
        return carry

    lax.fori_loop(0, rows // unroll, add_rows, 0)
    fold_by = LANES // orbs
    high = parts * projs // fold_by
    for slab in range(window_slabs):
        for atom in range(atoms):
            whole = acc[slab * atoms + atom]
            outs[slab][atom] = jnp.concatenate(
                [whole[k * high : (k + 1) * high] for k in range(fold_by)], axis=1
            )


def window_sums(
    local_cells, window_ids, cell_scale, quad_weights, proj_values, gradient_matrix, orbitals, atoms
):
    rows, projs, nodes = proj_values.shape
    cells, orbs, _ = orbitals.shape
    window_slabs = 2 * REACH + 1
    parts = 1 + gradient_matrix.shape[1] // nodes
    packed = (atoms, parts * projs * orbs // LANES, LANES)
    smem = pl.BlockSpec(memory_space=pltpu.SMEM)
    vmem = pl.BlockSpec(memory_space=pltpu.VMEM)
    flops = 2 * rows * projs * nodes * (nodes * (parts - 1) + orbs * parts)
    return pl.pallas_call(
        functools.partial(force_kernel, window_slabs=window_slabs, chunk=32, unroll=8),
        out_shape=[jax.ShapeDtypeStruct(packed, jnp.float32)] * window_slabs,
        in_specs=[smem, smem, smem, vmem, vmem, vmem, pl.BlockSpec(memory_space=pl.ANY)],
        out_specs=[vmem] * window_slabs,
        scratch_shapes=[
            pltpu.VMEM((rows, parts, projs, nodes), jnp.bfloat16),
            pltpu.VMEM(orbitals.shape, jnp.bfloat16),
            pltpu.VMEM((window_slabs * atoms + 1, parts * projs, orbs), jnp.float32),
            pltpu.SemaphoreType.DMA,
        ],
        cost_estimate=pl.CostEstimate(
            flops=flops, bytes_accessed=2 * orbitals.size + 2 * proj_values.size, transcendentals=0
        ),
        name="window_sums",
    )(
        local_cells,
        window_ids,
        cell_scale,
        quad_weights.reshape(1, nodes),
        proj_values,
        gradient_matrix,
        orbitals,
    )


def stress_kernel(
    weight_ref, scale_ref, matrix_ref, orbitals_ref, out_ref, even, odd, sums, *, block
):
    step = pl.program_id(0)
    orbs, nodes = weight_ref.shape
    cells = out_ref.shape[1]

    def gradient(half, buffer):
        flat = orbitals_ref[half * block : (half + 1) * block].reshape(block * orbs, nodes)
        buffer[...] = jnp.dot(flat, matrix_ref[...], preferred_element_type=jnp.float32)

    def reduce(buffer, first_row):
        totals = [[] for _ in PAIRS]
        for cell in range(block):
            acc = [None] * len(PAIRS)
            for group in range(orbs // 8):
                row = cell * orbs + group * 8
                weight = weight_ref[group * 8 : group * 8 + 8, :]
                grad = [buffer[row : row + 8, i * nodes : (i + 1) * nodes] for i in range(3)]
                scaled = [weight * grad[i] for i in range(3)]
                for k, (i, j) in enumerate(PAIRS):
                    term = scaled[i] * grad[j]
                    acc[k] = term if acc[k] is None else acc[k] + term
            for k in range(len(PAIRS)):
                lanes = acc[k][:, :LANES]
                for c in range(1, nodes // LANES):
                    lanes = lanes + acc[k][:, c * LANES : (c + 1) * LANES]
                totals[k].append(jnp.sum(lanes, axis=0, keepdims=True))
        at = pl.ds(pl.multiple_of(first_row, block), block)
        for k in range(len(PAIRS)):
            sums[k, at, :] = jnp.concatenate(totals[k], axis=0)

    gradient(0, even)
    reduce(odd, 2 * step * block)
    gradient(1, odd)
    reduce(even, (2 * step + 1) * block)

    @pl.when(step == pl.num_programs(0) - 1)
    def finish():
        reduce(odd, cells)
        ones = jnp.ones((8, LANES), jnp.float32)
        whole = [
            lax.dot_general(
                ones,
                sums[k, block:, :],
                CONTRACT_LAST,
                precision=lax.Precision.HIGHEST,
                preferred_element_type=jnp.float32,
            )[:1]
            for k in range(len(PAIRS))
        ]
        half = 0.5 * (whole[0] + whole[1] + whole[2])
        square = scale_ref[...] * scale_ref[...]
        for k in range(3):
            out_ref[k : k + 1, :] = (half - whole[k]) * square
        for k in range(3, 6):
            out_ref[k : k + 1, :] = -whole[k] * square


def stress_sums(weighting, cell_scale, gradient_matrix, orbitals):
    cells, orbs, nodes = orbitals.shape
    block = 512 // orbs
    columns = gradient_matrix.shape[1]
    whole = lambda shape: pl.BlockSpec(shape, lambda t: (0,) * len(shape))
    return pl.pallas_call(
        functools.partial(stress_kernel, block=block),
        grid=(cells // (2 * block),),
        out_shape=jax.ShapeDtypeStruct((6, cells), jnp.float32),
        in_specs=[
            whole((orbs, nodes)),
            whole((1, cells)),
            whole((nodes, columns)),
            pl.BlockSpec((2 * block, orbs, nodes), lambda t: (t, 0, 0)),
        ],
        out_specs=whole((6, cells)),
        scratch_shapes=[
            pltpu.VMEM((block * orbs, columns), jnp.float32),
            pltpu.VMEM((block * orbs, columns), jnp.float32),
            pltpu.VMEM((6, cells + block, LANES), jnp.float32),
        ],
        cost_estimate=pl.CostEstimate(
            flops=2 * orbitals.size * columns, bytes_accessed=2 * orbitals.size, transcendentals=0
        ),
        name="stress_sums",
    )(weighting, cell_scale.reshape(1, cells), gradient_matrix, orbitals)


def local(
    orbitals,
    gradient_matrix,
    quad_weights,
    cell_scale,
    occupations,
    support_cell,
    support_atom,
    proj_values,
    proj_coupling,
):
    cell_count, orbital_count, node_count = orbitals.shape
    proj_count = proj_values.shape[1]
    atom_total = proj_coupling.shape[0]
    slab_total = lax.axis_size("cells")
    atom_share = atom_total // slab_total
    window_slabs = 2 * REACH + 1
    slab_index = lax.axis_index("cells")
    orbital_total = orbital_count * lax.axis_size("orb")

    local_cells = support_cell - slab_index * cell_count
    live_atom = jnp.maximum(support_atom, 0)
    relative = jnp.mod(live_atom // atom_share - slab_index + REACH, slab_total)
    window_ids = relative * atom_share + jnp.mod(live_atom, atom_share)
    window_ids = jnp.where(support_atom >= 0, window_ids, window_slabs * atom_share)

    parts = window_sums(
        local_cells,
        window_ids,
        cell_scale,
        quad_weights,
        proj_values,
        gradient_matrix,
        orbitals,
        atom_share,
    )
    owned = parts[REACH]
    for offset in range(-REACH, REACH + 1):
        if offset != 0:
            owned = owned + from_behind(parts[offset + REACH], "cells", offset)

    weighting = occupations[:, None] * quad_weights[None, :] / orbital_total
    stress_part = stress_sums(weighting, cell_scale, gradient_matrix, orbitals)

    fold_by = LANES // orbital_count
    owned = jnp.concatenate(
        [owned[:, :, k * orbital_count : (k + 1) * orbital_count] for k in range(fold_by)], axis=1
    )
    owned = owned.reshape(atom_share, 4, proj_count, orbital_count)
    coupling = lax.dynamic_slice_in_dim(proj_coupling, slab_index * atom_share, atom_share, 0)
    weight_terms = coupling[:, :, None] * occupations[None, None, :]
    force_part = -2.0 * jnp.sum(owned[:, 1:] * (owned[:, 0] * weight_terms)[:, None], axis=(2, 3))
    eshelby, forces = lax.psum((stress_part, jnp.transpose(force_part)), "orb")
    return (eshelby, forces)


def solution(mesh):
    return jax.shard_map(
        local,
        mesh=mesh,
        in_specs=(
            P("cells", "orb", None),
            P(),
            P(),
            P("cells"),
            P("orb"),
            P("cells"),
            P("cells"),
            P("cells", None, None),
            P(),
        ),
        out_specs=(P(None, "cells"), P(None, "cells")),
        check_vma=False,
    )
```

time: 337 us -> 50.3 us (0.15)
  local copies, waits for them, and re-layouts: 220 us -> 1 us
  matrix products: 51.2 us -> 0 us
  Pallas kernels: 0 us -> 31.7 us
  other arithmetic: 32.1 us -> 2.22 us
  waiting for transfers between devices: 14.4 us -> 0.01 us
    broadcast_in_dim x8 -> x0, local copies, waits for them, and re-layouts: 66.7 us -> none  [local(): stress_blocks, stored_blocks = lax.map(cell_block, blocked)]
    gather x4 -> x0, local copies, waits for them, and re-layouts: 64.4 us -> none  [the longest x2 53.2 us: add_block(): stored[local_cells].reshape(BLOCK, orbital_count, 3, node_count)]
    dot_general x11 -> x0, matrix products: 51.2 us -> none  [the longest x8 28.4 us: cell_block(): jnp.dot(block_orbitals.reshape(-1, node_count), gradient_matrix, preferre...]
    convert_element_type x8 -> x0, local copies, waits for them, and re-layouts: 37.6 us -> none  [cell_block(): gradient.astype(jnp.bfloat16)]
    reshape x3 -> x0, local copies, waits for them, and re-layouts: 32.1 us -> none  [the longest x1 31.3 us: add_block(): stored[local_cells].reshape(BLOCK, orbital_count, 3, node_count)]
    pallas_call x0 -> x2, Pallas kernels: none -> 31.7 us  [the longest x1 19.8 us: stress_sums(): pl.pallas_call(functools.partial(stress_kernel, block=block), grid=(cells...]
    reduce_sum x9 -> x1, other arithmetic: 29.4 us -> 0.13 us  [local(): jnp.sum(owned[:, 1:] * (owned[:, 0] * weight_terms)[:, None], axis=(2, 3))]
    dynamic_update_slice x16 -> x0, local copies, waits for them, and re-layouts: 15.8 us -> none  [local(): stress_blocks, stored_blocks = lax.map(cell_block, blocked)]
  transfers between devices with their start and end apart: 4 -> 4, of which waited for: 3 -> 0; matrix products, arithmetic and copies ran while one was open for 0% -> 2% of each run, Pallas kernels for 0% -> 39%
where the time goes in v1:
time: 50.3 us; the launch traced here: 50.1 us
  Pallas kernels  31.7 us (63%)
  starting transfers between devices  8.12 us (16%)
  blocking collectives  6.39 us (13%)
  other arithmetic  2.22 us (4%)
  local copies, waits for them, and re-layouts  1 us (2%)
  between operations  0.72 us (1%)
    pallas_call x1, Pallas kernels, stress_sums(): pl.pallas_call(functools.partial(stress_kernel, block=block), grid=(cells...  19.8 us
    pallas_call x1, Pallas kernels, window_sums(): pl.pallas_call(functools.partial(force_kernel, window_slabs=window_slabs,...  11.9 us
    ppermute x4, starting transfers between devices, from_behind(): lax.ppermute(shard, axis, [(i, (i + by) % length) for i in range(length)])  8.12 us
    psum x1, blocking collectives, local(): eshelby, forces = lax.psum((stress_part, jnp.transpose(force_part)), 'orb')  6.39 us
    select_n x1, other arithmetic, local(): jnp.where(support_atom >= 0, window_ids, window_slabs * atom_share)  1.2 us
  transfers between devices with their start and end apart: 4, of which 0 were waited for; matrix products, arithmetic and copies ran while one was open for 2% of the time, Pallas kernels for 39%

profile of v1, /device:TPU:0, one launch (start us, length us, event | category | flops | bytes accessed | tf_op | source)
XLA Modules:
  0.0 50.1 jit_solution(2292955534434248435)
XLA Ops:
  0.6 0.0 copy-start
  0.7 1.2 %compare_select_fusion.2 = (s32[128]{0:T(128)}, s32[128]{0:T(128)}) fusion(s32[128]{0:T(128)} %param.15, s32[]{:T(128)S(6)} %axis_index.15, s32[128]{0:T(128)} %param.14, s32[]{:T(128)S(6)} %mul.67), kind=kLoop, calls=%fused_computation.13 | loop fusion | flops 3968 | bytes 2056 | tf_op jit(solution)/shard_map/jit(_where)/select_n | solution.py:236
  1.9 0.0 copy-start.3
  1.9 0.0 copy-start.4
  1.9 11.9 %window_sums.1 = (f32[8,32,128]{2,1,0:T(8,128)}, f32[8,32,128]{2,1,0:T(8,128)}, f32[8,32,128]{2,1,0:T(8,128)}, f32[8,32,128]{2,1,0:T(8,128)}, f32[8,32,128]{2,1,0:T(8,128)}) custom-call(s32[128]{0:T(128)} %get-tuple-element.19.cell_ref, s32[128]{0:T(128)} %get-tuple-element.18.window_ref, f32[128]{0:T(128)} %scale_ref.1, f32[1,512]{1,0:T(1,128)} %bitcast.9, ...), custom_call_target="tpu_custom_call" | custom-call | flops 3758096384 | bytes 10485760 | tf_op jit(solution)/shard_map/window_sums/pallas_call | solution.py:99
  13.8 5.1 %collective-permute-start = (f32[8,32,128]{2,1,0:T(8,128)}, f32[8,32,128]{2,1,0:T(8,128)S(1)}, u32[]{:S(2)}, u32[]{:S(2)}) collective-permute-start(f32[8,32,128]{2,1,0:T(8,128)} %get-tuple-element.8), channel_id=1, source_target_pairs={{0,24},{4,28},{8,0},{12,4},{16,8},{20,12},{24,16},{28,20},{1,25},{... | collective-permute-start | bytes 393224 | tf_op jit(solution)/shard_map/ppermute | solution.py:18
  18.9 1.4 %collective-permute-start.1 = (f32[8,32,128]{2,1,0:T(8,128)}, f32[8,32,128]{2,1,0:T(8,128)S(1)}, u32[]{:S(2)}, u32[]{:S(2)}) collective-permute-start(f32[8,32,128]{2,1,0:T(8,128)} %get-tuple-element.9), channel_id=1, source_target_pairs={{0,28},{4,0},{8,4},{12,8},{16,12},{20,16},{24,20},{28,24},{1,29},{... | collective-permute-start | bytes 393224 | tf_op jit(solution)/shard_map/ppermute | solution.py:18
  20.3 0.7 %collective-permute-start.2 = (f32[8,32,128]{2,1,0:T(8,128)}, f32[8,32,128]{2,1,0:T(8,128)S(1)}, u32[]{:S(2)}, u32[]{:S(2)}) collective-permute-start(f32[8,32,128]{2,1,0:T(8,128)} %get-tuple-element.10), channel_id=1, source_target_pairs={{0,4},{4,8},{8,12},{12,16},{16,20},{20,24},{24,28},{28,0},{1,5},{5... | collective-permute-start | bytes 393224 | tf_op jit(solution)/shard_map/ppermute | solution.py:18
  20.9 1.0 %collective-permute-start.3 = (f32[8,32,128]{2,1,0:T(8,128)}, f32[8,32,128]{2,1,0:T(8,128)S(1)}, u32[]{:S(2)}, u32[]{:S(2)}) collective-permute-start(f32[8,32,128]{2,1,0:T(8,128)} %get-tuple-element.11), channel_id=1, source_target_pairs={{0,8},{4,12},{8,16},{12,20},{16,24},{20,28},{24,0},{28,4},{1,9},{5... | collective-permute-start | bytes 393224 | tf_op jit(solution)/shard_map/ppermute | solution.py:18
  21.9 0.0 copy-done.3
  21.9 0.0 copy-done.4
  21.9 0.7 %multiply_multiply_fusion.weight_ref = f32[64,512]{1,0:T(8,128)} fusion(f32[512]{0:T(512)S(1)} %copy-done.3, f32[64]{0:T(128)S(1)} %copy-done.4), kind=kLoop, calls=%fused_computation.4 | loop fusion | flops 65536 | bytes 133376 | tf_op jit(solution)/shard_map/div | solution.py:253
  22.6 0.0 copy-start.1
  22.6 19.8 %stress_sums.1 = f32[6,128]{1,0:T(8,128)} custom-call(f32[64,512]{1,0:T(8,128)} %multiply_multiply_fusion.weight_ref, f32[1,128]{1,0:T(1,128)} %bitcast.10, bf16[512,1536]{1,0:T(8,128)(2,1)} %matrix_ref.3, bf16[128,64,512]{2,1,0:T(8,128)(2,1)} %orbitals_hbm.1), custom_call_target="tpu_custom_call" | custom-call | flops 12884901888 | bytes 8388608 | tf_op jit(solution)/shard_map/stress_sums/pallas_call | solution.py:189
  42.4 0.0 copy-start.2
  42.4 0.0 copy-done
  42.4 0.1 constant_dynamic-slice_fusion
  42.5 0.1 copy.12
  42.5 0.0 collective-permute-done
  42.5 0.0 collective-permute-done.1
  42.5 0.0 collective-permute-done.2
  42.6 0.0 collective-permute-done.3
  42.6 0.0 copy-done.1
  42.6 0.1 fusion.5
  42.8 0.1 fusion.1
  42.9 0.1 fusion
  43.0 0.1 copy-done.2
  43.1 6.4 %all-reduce = (f32[6,128]{1,0:T(8,128)}, f32[3,8]{0,1:T(8,128)S(1)}) all-reduce(f32[6,128]{1,0:T(8,128)S(1)} %copy-done.2, f32[3,8]{0,1:T(8,128)S(1)} %multiply_bitcast_fusion), channel_id=1, replica_groups=mesh['cells'=8,'orb'=4] {'orb'}, use_global_device_ids=true, to_apply=%region_0.1 | all-reduce | flops 792 | bytes 6336 | tf_op jit(solution)/shard_map/psum | solution.py:264
  49.5 0.7 %copy.13 = f32[3,8]{1,0:T(4,128)} copy(f32[3,8]{0,1:T(8,128)S(1)} %get-tuple-element.15) | data formatting | bytes 192
  (3 shorter events, 0.1 us)
Async XLA Ops:
  0.6 41.8 %copy-start = (f32[64,16]{0,1:T(8,128)S(1)}, f32[64,16]{0,1:T(8,128)}, u32[]{:S(2)}) copy-start(f32[64,16]{0,1:T(8,128)} %param.17) | copy-start | bytes 12292
  1.9 20.0 %copy-start.3 = (f32[512]{0:T(512)S(1)}, f32[512]{0:T(512)}, u32[]{:S(2)}) copy-start(f32[512]{0:T(512)} %param.11) | copy-start | bytes 6148
  1.9 20.0 %copy-start.4 = (f32[64]{0:T(128)S(1)}, f32[64]{0:T(128)}, u32[]{:S(2)}) copy-start(f32[64]{0:T(128)} %param.13) | copy-start | bytes 772
  13.8 28.8 %collective-permute-start = (f32[8,32,128]{2,1,0:T(8,128)}, f32[8,32,128]{2,1,0:T(8,128)S(1)}, u32[]{:S(2)}, u32[]{:S(2)}) collective-permute-start(f32[8,32,128]{2,1,0:T(8,128)} %get-tuple-element.8), channel_id=1, source_target_pairs={{0,24},{4,28},{8,0},{12,4},{16,8},{20,12},{24,16},{28,20},{1,25},{... | collective-permute-start | bytes 393224 | tf_op jit(solution)/shard_map/ppermute | solution.py:18
  18.9 23.6 %collective-permute-start.1 = (f32[8,32,128]{2,1,0:T(8,128)}, f32[8,32,128]{2,1,0:T(8,128)S(1)}, u32[]{:S(2)}, u32[]{:S(2)}) collective-permute-start(f32[8,32,128]{2,1,0:T(8,128)} %get-tuple-element.9), channel_id=1, source_target_pairs={{0,28},{4,0},{8,4},{12,8},{16,12},{20,16},{24,20},{28,24},{1,29},{... | collective-permute-start | bytes 393224 | tf_op jit(solution)/shard_map/ppermute | solution.py:18
  20.3 22.3 %collective-permute-start.2 = (f32[8,32,128]{2,1,0:T(8,128)}, f32[8,32,128]{2,1,0:T(8,128)S(1)}, u32[]{:S(2)}, u32[]{:S(2)}) collective-permute-start(f32[8,32,128]{2,1,0:T(8,128)} %get-tuple-element.10), channel_id=1, source_target_pairs={{0,4},{4,8},{8,12},{12,16},{16,20},{20,24},{24,28},{28,0},{1,5},{5... | collective-permute-start | bytes 393224 | tf_op jit(solution)/shard_map/ppermute | solution.py:18
  20.9 21.6 %collective-permute-start.3 = (f32[8,32,128]{2,1,0:T(8,128)}, f32[8,32,128]{2,1,0:T(8,128)S(1)}, u32[]{:S(2)}, u32[]{:S(2)}) collective-permute-start(f32[8,32,128]{2,1,0:T(8,128)} %get-tuple-element.11), channel_id=1, source_target_pairs={{0,8},{4,12},{8,16},{12,20},{16,24},{20,28},{24,0},{28,4},{1,9},{5... | collective-permute-start | bytes 393224 | tf_op jit(solution)/shard_map/ppermute | solution.py:18
  22.6 20.0 %copy-start.1 = (f32[8,32,128]{2,1,0:T(8,128)S(1)}, f32[8,32,128]{2,1,0:T(8,128)}, u32[]{:S(2)}) copy-start(f32[8,32,128]{2,1,0:T(8,128)} %get-tuple-element.7) | copy-start | bytes 393220
  42.4 0.7 %copy-start.2 = (f32[6,128]{1,0:T(8,128)S(1)}, f32[6,128]{1,0:T(8,128)}, u32[]{:S(2)}) copy-start(f32[6,128]{1,0:T(8,128)} %stress_sums.1) | copy-start | bytes 9220

commit v2 on v1

v2 whole, which is shorter than its diff:
```python
import functools
import math

import jax
import jax.numpy as jnp
from jax import lax
from jax.experimental import pallas as pl
from jax.experimental.pallas import tpu as pltpu
from jax.sharding import PartitionSpec as P

REACH = 2
LANES = 128
SUBLANES = 8
PAIRS = ((0, 0), (1, 1), (2, 2), (0, 1), (0, 2), (1, 2))
CONTRACT_LAST = (((1,), (1,)), ((), ()))
FORCE_MIB, STRESS_MIB = 28, 30
SMEM = pl.BlockSpec(memory_space=pltpu.SMEM)
VMEM = pl.BlockSpec(memory_space=pltpu.VMEM)
HBM = pl.BlockSpec(memory_space=pltpu.HBM)


def from_behind(shard, axis, by):
    length = lax.axis_size(axis)
    return lax.ppermute(shard, axis, [(i, (i + by) % length) for i in range(length)])


def force_kernel(
    cell_hbm,
    atom_hbm,
    scale_hbm,
    quad_hbm,
    proj_hbm,
    matrix_hbm,
    orbitals_hbm,
    *rest,
    window_slabs,
    slab_total,
    chunk,
    unroll,
):
    outs = rest[:window_slabs]
    matrix_ref, orbitals_ref, quad_ref, proj_ref, folded, acc = rest[window_slabs : window_slabs + 6]
    cell_ref, atom_ref, scale_ref, sems, small_sems = rest[window_slabs + 6 :]
    rows, parts, projs, nodes = folded.shape
    atoms = outs[0].shape[0]
    cells, orbs, _ = orbitals_ref.shape
    slab = lax.axis_index("cells")
    chunks = rows // chunk

    def columns(i):
        return pl.ds(i * nodes, nodes)

    load_quad = pltpu.make_async_copy(quad_hbm, quad_ref, sems.at[0])
    load_matrix = [
        pltpu.make_async_copy(
            matrix_hbm.at[:, columns(i)], matrix_ref.at[:, columns(i)], sems.at[1 + i]
        )
        for i in range(parts - 1)
    ]
    load_proj = [
        pltpu.make_async_copy(
            proj_hbm.at[pl.ds(c * chunk, chunk)],
            proj_ref.at[pl.ds(c * chunk, chunk)],
            sems.at[parts + c],
        )
        for c in range(chunks)
    ]
    load_orbitals = pltpu.make_async_copy(orbitals_hbm, orbitals_ref, sems.at[parts + chunks])
    load_small = [
        pltpu.make_async_copy(source, target, small_sems.at[k])
        for k, (source, target) in enumerate(
            ((cell_hbm, cell_ref), (atom_hbm, atom_ref), (scale_hbm, scale_ref))
        )
    ]
    load_quad.start()
    load_proj[0].start()
    for load in load_matrix:
        load.start()
    for load in load_proj[1:]:
        load.start()
    for load in load_small:
        load.start()
    acc[...] = jnp.zeros_like(acc)
    load_quad.wait()
    load_proj[0].wait()
    load_orbitals.start()

    for c in range(chunks):
        if c > 0:
            load_proj[c].wait()
        at = pl.ds(c * chunk, chunk)
        scaled = (proj_ref[at].astype(jnp.float32) * quad_ref[...][None]).astype(jnp.bfloat16)
        folded[at, 0] = scaled
        flat = scaled.reshape(chunk * projs, nodes)
        for i in range(parts - 1):
            if c == 0:
                load_matrix[i].wait()
            part = lax.dot_general(
                flat,
                matrix_ref[:, i * nodes : (i + 1) * nodes],
                CONTRACT_LAST,
                preferred_element_type=jnp.float32,
            )
            folded[at, i + 1] = part.astype(jnp.bfloat16).reshape(chunk, projs, nodes)
    load_orbitals.wait()
    for load in load_small:
        load.wait()

    def place(row):
        atom = atom_ref[row]
        owner = lax.div(jnp.maximum(atom, 0), atoms)
        relative = owner - slab + REACH
        relative = jnp.where(relative < 0, relative + slab_total, relative)
        relative = jnp.where(relative >= slab_total, relative - slab_total, relative)
        slot = (relative - owner) * atoms + atom
        return jnp.where(atom < 0, window_slabs * atoms, slot)

    def add_rows(step, carry):
        terms = []
        for j in range(unroll):
            row = step * unroll + j
            cell = cell_ref[row] - slab * cells
            term = lax.dot_general(
                folded[row].reshape(parts * projs, nodes),
                orbitals_ref[cell],
                CONTRACT_LAST,
                preferred_element_type=jnp.float32,
            )
            terms.append((place(row), scale_ref[cell], term))
        for slot, factor, term in terms:
            acc[slot, :projs] += term[:projs]
            acc[slot, projs:] += term[projs:] * factor
        return carry

    lax.fori_loop(0, rows // unroll, add_rows, 0)
    fold_by = LANES // orbs
    high = parts * projs // fold_by
    for window in range(window_slabs):
        for atom in range(atoms):
            whole = acc[window * atoms + atom]
            outs[window][atom] = jnp.concatenate(
                [whole[k * high : (k + 1) * high] for k in range(fold_by)], axis=1
            )


def window_sums(
    support_cell, support_atom, cell_scale, quad_weights, proj_values, gradient_matrix, orbitals, atoms, slab_total
):
    rows, projs, nodes = proj_values.shape
    cells, orbs, _ = orbitals.shape
    window_slabs = 2 * REACH + 1
    parts = 1 + gradient_matrix.shape[1] // nodes
    packed = (atoms, parts * projs * orbs // LANES, LANES)
    chunk = math.gcd(rows, 64)
    flops = 2 * rows * projs * nodes * (nodes * (parts - 1) + orbs * parts)
    results = pl.pallas_call(
        functools.partial(
            force_kernel,
            window_slabs=window_slabs,
            slab_total=slab_total,
            chunk=chunk,
            unroll=chunk,
        ),
        out_shape=[jax.ShapeDtypeStruct(packed, jnp.float32)] * window_slabs
        + [
            jax.ShapeDtypeStruct(gradient_matrix.shape, jnp.bfloat16),
            jax.ShapeDtypeStruct(orbitals.shape, jnp.bfloat16),
        ],
        in_specs=[HBM] * 7,
        out_specs=[VMEM] * (window_slabs + 2),
        compiler_params=pltpu.CompilerParams(vmem_limit_bytes=FORCE_MIB << 20),
        scratch_shapes=[
            pltpu.VMEM((1, nodes), jnp.float32),
            pltpu.VMEM(proj_values.shape, jnp.bfloat16),
            pltpu.VMEM((rows, parts, projs, nodes), jnp.bfloat16),
            pltpu.VMEM((window_slabs * atoms + 1, parts * projs, orbs), jnp.float32),
            pltpu.SMEM((rows,), jnp.int32),
            pltpu.SMEM((rows,), jnp.int32),
            pltpu.SMEM((cells,), jnp.float32),
            pltpu.SemaphoreType.DMA((parts + rows // chunk + 1,)),
            pltpu.SemaphoreType.DMA((3,)),
        ],
        cost_estimate=pl.CostEstimate(
            flops=flops, bytes_accessed=2 * orbitals.size + 2 * proj_values.size, transcendentals=0
        ),
        name="window_sums",
    )(
        *(
            pltpu.with_memory_space_constraint(operand, pltpu.HBM)
            for operand in (
                support_cell,
                support_atom,
                cell_scale,
                quad_weights.reshape(1, nodes),
                proj_values,
                gradient_matrix,
                orbitals,
            )
        )
    )
    return results[:window_slabs], results[window_slabs], results[window_slabs + 1]


def stress_kernel(
    occ_ref,
    quad_ref,
    scale_ref,
    matrix_ref,
    orbitals_ref,
    out_ref,
    even,
    odd,
    weight_ref,
    sums,
    *,
    share,
    block,
):
    orbs, nodes = weight_ref.shape
    cells = out_ref.shape[1]
    blocks = cells // block

    across = jnp.broadcast_to(occ_ref[...], (orbs, orbs))
    rows = lax.broadcasted_iota(jnp.int32, (orbs, orbs), 0)
    columns = lax.broadcasted_iota(jnp.int32, (orbs, orbs), 1)
    down = jnp.sum(jnp.where(rows == columns, across, 0.0), axis=1, keepdims=True)
    weight_ref[...] = down * quad_ref[...] * share

    def gradient_part(i, buffer, part):
        at = slice(part * nodes, (part + 1) * nodes)
        flat = orbitals_ref[pl.ds(pl.multiple_of(i * block, block), block)]
        buffer[:, at] = jnp.dot(
            flat.reshape(block * orbs, nodes), matrix_ref[:, at], preferred_element_type=jnp.float32
        )

    def reduce_cells(buffer, first, last, totals):
        for cell in range(first, last):
            acc = [None] * len(PAIRS)
            for group in range(orbs // SUBLANES):
                at = slice(group * SUBLANES, (group + 1) * SUBLANES)
                row = cell * orbs + group * SUBLANES
                weight = weight_ref[at, :]
                grad = [
                    buffer[row : row + SUBLANES, i * nodes : (i + 1) * nodes] for i in range(3)
                ]
                scaled = [weight * grad[i] for i in range(3)]
                for k, (a, b) in enumerate(PAIRS):
                    term = scaled[a] * grad[b]
                    acc[k] = term if acc[k] is None else acc[k] + term
            for k in range(len(PAIRS)):
                lanes = acc[k][:, :LANES]
                for c in range(1, nodes // LANES):
                    lanes = lanes + acc[k][:, c * LANES : (c + 1) * LANES]
                totals[k].append(jnp.sum(lanes, axis=0, keepdims=True))

    def store(i, totals):
        at = pl.ds(pl.multiple_of(i * block, block), block)
        for k in range(len(PAIRS)):
            sums[k, at, :] = jnp.concatenate(totals[k], axis=0)

    def both(i, full, empty):
        totals = [[] for _ in PAIRS]
        for part in range(3):
            reduce_cells(full, part * block // 3, (part + 1) * block // 3, totals)
            gradient_part(i + 1, empty, part)
        store(i, totals)

    for part in range(3):
        gradient_part(0, even, part)

    def pair(t, carry):
        both(2 * t, even, odd)
        both(2 * t + 1, odd, even)
        return carry

    lax.fori_loop(0, blocks // 2 - 1, pair, 0)
    both(blocks - 2, even, odd)
    totals = [[] for _ in PAIRS]
    reduce_cells(odd, 0, block, totals)
    store(blocks - 1, totals)

    whole = [jnp.sum(jnp.transpose(sums[k]), axis=0, keepdims=True) for k in range(len(PAIRS))]
    half = 0.5 * (whole[0] + whole[1] + whole[2])
    square = scale_ref[...] * scale_ref[...]
    for k in range(3):
        out_ref[k : k + 1, :] = (half - whole[k]) * square
    for k in range(3, 6):
        out_ref[k : k + 1, :] = -whole[k] * square


def stress_sums(occupations, quad_weights, cell_scale, gradient_matrix, orbitals, orbital_total):
    cells, orbs, nodes = orbitals.shape
    block = min(1024 // orbs, cells // 2)
    columns = gradient_matrix.shape[1]
    return pl.pallas_call(
        functools.partial(stress_kernel, share=1.0 / orbital_total, block=block),
        out_shape=jax.ShapeDtypeStruct((6, cells), jnp.float32),
        in_specs=[VMEM, VMEM, VMEM, VMEM, VMEM],
        out_specs=VMEM,
        compiler_params=pltpu.CompilerParams(vmem_limit_bytes=STRESS_MIB << 20),
        scratch_shapes=[
            pltpu.VMEM((block * orbs, columns), jnp.float32),
            pltpu.VMEM((block * orbs, columns), jnp.float32),
            pltpu.VMEM((orbs, nodes), jnp.float32),
            pltpu.VMEM((6, cells, LANES), jnp.float32),
        ],
        cost_estimate=pl.CostEstimate(
            flops=2 * orbitals.size * columns, bytes_accessed=2 * orbitals.size, transcendentals=0
        ),
        name="stress_sums",
    )(
        occupations.reshape(1, orbs),
        quad_weights.reshape(1, nodes),
        cell_scale.reshape(1, cells),
        gradient_matrix,
        orbitals,
    )


def local(
    orbitals,
    gradient_matrix,
    quad_weights,
    cell_scale,
    occupations,
    support_cell,
    support_atom,
    proj_values,
    proj_coupling,
):
    cells, orbital_count, node_count = orbitals.shape
    proj_count = proj_values.shape[1]
    atom_total = proj_coupling.shape[0]
    slab_total = lax.axis_size("cells")
    atom_share = atom_total // slab_total
    slab_index = lax.axis_index("cells")
    orbital_total = orbital_count * lax.axis_size("orb")

    parts, near_matrix, near_orbitals = window_sums(
        support_cell,
        support_atom,
        cell_scale,
        quad_weights,
        proj_values,
        gradient_matrix,
        orbitals,
        atom_share,
        slab_total,
    )
    owned = parts[REACH]
    for offset in range(-REACH, REACH + 1):
        if offset != 0:
            owned = owned + from_behind(parts[offset + REACH], "cells", offset)

    stress_part = stress_sums(
        occupations, quad_weights, cell_scale, near_matrix, near_orbitals, orbital_total
    )

    fold_by = LANES // orbital_count
    owned = jnp.concatenate(
        [owned[:, :, k * orbital_count : (k + 1) * orbital_count] for k in range(fold_by)], axis=1
    )
    owned = owned.reshape(atom_share, 4, proj_count, orbital_count)
    coupling = lax.dynamic_slice_in_dim(proj_coupling, slab_index * atom_share, atom_share, 0)
    weight_terms = coupling[:, :, None] * occupations[None, None, :]
    force_part = -2.0 * jnp.sum(owned[:, 1:] * (owned[:, 0] * weight_terms)[:, None], axis=(2, 3))
    force_part = jnp.pad(
        jnp.transpose(force_part), ((0, SUBLANES - 3), (0, cells - atom_share))
    )
    packed = jnp.concatenate([stress_part, jnp.zeros((2, cells), jnp.float32), force_part], axis=0)
    copies = [packed] + [from_behind(packed, "orb", by) for by in range(1, lax.axis_size("orb"))]
    total = functools.reduce(jnp.add, copies)
    return (total[:6], total[8:11, :atom_share])


def solution(mesh):
    return jax.shard_map(
        local,
        mesh=mesh,
        in_specs=(
            P("cells", "orb", None),
            P(),
            P(),
            P("cells"),
            P("orb"),
            P("cells"),
            P("cells"),
            P("cells", None, None),
            P(),
        ),
        out_specs=(P(None, "cells"), P(None, "cells")),
        check_vma=False,
    )
```

time: 50.3 us -> 41.3 us (0.82)
  blocking collectives: 6.39 us -> 0 us
  Pallas kernels: 31.7 us -> 25.6 us
  waiting for transfers between devices: 0.01 us -> 2.58 us
  starting transfers between devices: 8.12 us -> 10.1 us
  other arithmetic: 2.22 us -> 0.45 us
  local copies, waits for them, and re-layouts: 1 us -> 1.59 us
    psum x1 -> x0, blocking collectives: 6.39 us -> none  [local(): eshelby, forces = lax.psum((stress_part, jnp.transpose(force_part)), 'orb')]
    pallas_call x1, Pallas kernels: 11.9 us -> 8.47 us  [window_sums(): pl.pallas_call(functools.partial(force_kernel, window_slabs=window_slabs,...]
    pallas_call x1, Pallas kernels: 19.8 us -> 17.2 us  [stress_sums(): pl.pallas_call(functools.partial(stress_kernel, share=1.0 / orbital_total...]
    ppermute x4 -> x7, waiting for transfers between devices: 0.01 us -> 2.58 us  [from_behind(): lax.ppermute(shard, axis, [(i, (i + by) % length) for i in range(length)])]
    ppermute x4 -> x7, starting transfers between devices: 8.12 us -> 10.1 us  [from_behind(): lax.ppermute(shard, axis, [(i, (i + by) % length) for i in range(length)])]
    select_n x1 -> x0, other arithmetic: 1.2 us -> none  [local(): jnp.where(support_atom >= 0, window_ids, window_slabs * atom_share)]
    slice x0 -> x2, local copies, waits for them, and re-layouts: none -> 1.18 us  [local(): return (total[:6], total[8:11, :atom_share])]
    div x1 -> x0, other arithmetic: 0.73 us -> none  [local(): weighting = occupations[:, None] * quad_weights[None, :] / orbital_total]
  transfers between devices with their start and end apart: 4 -> 7, of which waited for: 0 -> 2; matrix products, arithmetic and copies ran while one was open for 2% -> 1% of each run, Pallas kernels for 39% -> 42%
where the time goes in v2:
time: 41.3 us; the launch traced here: 41.1 us
  Pallas kernels  25.6 us (62%)
  starting transfers between devices  10.1 us (24%)
  waiting for transfers between devices  2.58 us (6%)
  local copies, waits for them, and re-layouts  1.59 us (4%)
  between operations  0.74 us (2%)
  other arithmetic  0.45 us (1%)
    pallas_call x1, Pallas kernels, stress_sums(): pl.pallas_call(functools.partial(stress_kernel, share=1.0 / orbital_total...  17.2 us
    ppermute x7, starting transfers between devices, from_behind(): lax.ppermute(shard, axis, [(i, (i + by) % length) for i in range(length)])  10.1 us
    pallas_call x1, Pallas kernels, window_sums(): pl.pallas_call(functools.partial(force_kernel, window_slabs=window_slabs,...  8.47 us
    ppermute x7, waiting for transfers between devices, from_behind(): lax.ppermute(shard, axis, [(i, (i + by) % length) for i in range(length)])  2.58 us
    slice x2, local copies, waits for them, and re-layouts, local(): return (total[:6], total[8:11, :atom_share])  1.18 us
  transfers between devices with their start and end apart: 7, of which 2 were waited for; matrix products, arithmetic and copies ran while one was open for 1% of the time, Pallas kernels for 42%

profile of v2, /device:TPU:0, one launch (start us, length us, event | category | flops | bytes accessed | tf_op | source)
XLA Modules:
  0.0 41.1 jit_solution(16173047588351454126)
XLA Ops:
  0.6 0.0 copy-start
  0.6 0.0 copy-start.1
  0.7 0.0 copy-start.2
  0.7 0.0 copy-start.3
  0.7 8.5 %window_sums.1 = (f32[8,32,128]{2,1,0:T(8,128)S(1)}, f32[8,32,128]{2,1,0:T(8,128)S(1)}, f32[8,32,128]{2,1,0:T(8,128)S(1)}, f32[8,32,128]{2,1,0:T(8,128)S(1)}, f3...) custom-call(s32[128]{0:T(128)} %cell_hbm.1, s32[128]{0:T(128)} %atom_hbm.1, ...), custom_call_target="tpu_custom_call" | custom-call | flops 3758096384 | bytes 10485760 | tf_op jit(solution)/shard_map/window_sums/pallas_call | solution.py:156
  9.2 5.1 %collective-permute-start = (f32[8,32,128]{2,1,0:T(8,128)S(1)}, f32[8,32,128]{2,1,0:T(8,128)S(1)}, u32[]{:S(2)}, u32[]{:S(2)}) collective-permute-start(f32[8,32,128]{2,1,0:T(8,128)S(1)} %get-tuple-element.12), channel_id=1, source_target_pairs={{0,24},{4,28},{8,0},{12,4},{16,8},{20,12},{24,16},{28,20},{1,25},{... | collective-permute-start | bytes 393224 | tf_op jit(solution)/shard_map/ppermute | solution.py:24
  14.3 1.4 %collective-permute-start.1 = (f32[8,32,128]{2,1,0:T(8,128)S(1)}, f32[8,32,128]{2,1,0:T(8,128)S(1)}, u32[]{:S(2)}, u32[]{:S(2)}) collective-permute-start(f32[8,32,128]{2,1,0:T(8,128)S(1)} %get-tuple-element.13), channel_id=1, source_target_pairs={{0,28},{4,0},{8,4},{12,8},{16,12},{20,16},{24,20},{28,24},{1,29},{... | collective-permute-start | bytes 393224 | tf_op jit(solution)/shard_map/ppermute | solution.py:24
  15.7 0.6 %collective-permute-start.2 = (f32[8,32,128]{2,1,0:T(8,128)S(1)}, f32[8,32,128]{2,1,0:T(8,128)S(1)}, u32[]{:S(2)}, u32[]{:S(2)}) collective-permute-start(f32[8,32,128]{2,1,0:T(8,128)S(1)} %get-tuple-element.14), channel_id=1, source_target_pairs={{0,4},{4,8},{8,12},{12,16},{16,20},{20,24},{24,28},{28,0},{1,5},{5... | collective-permute-start | bytes 393224 | tf_op jit(solution)/shard_map/ppermute | solution.py:24
  16.3 1.0 %collective-permute-start.3 = (f32[8,32,128]{2,1,0:T(8,128)S(1)}, f32[8,32,128]{2,1,0:T(8,128)S(1)}, u32[]{:S(2)}, u32[]{:S(2)}) collective-permute-start(f32[8,32,128]{2,1,0:T(8,128)S(1)} %get-tuple-element.15), channel_id=1, source_target_pairs={{0,8},{4,12},{8,16},{12,20},{16,24},{20,28},{24,0},{28,4},{1,9},{5... | collective-permute-start | bytes 393224 | tf_op jit(solution)/shard_map/ppermute | solution.py:24
  17.3 0.0 copy-done.1
  17.3 0.0 copy-done.2
  17.3 0.0 copy-done.3
  17.3 17.2 %stress_sums.1 = f32[6,128]{1,0:T(8,128)S(1)} custom-call(f32[1,64]{1,0:T(1,128)S(1)} %bitcast.8, f32[1,512]{1,0:T(1,128)S(1)} %bitcast.10, f32[1,128]{1,0:T(1,128)S(1)} %bitcast.11, bf16[512,1536]{1,0:T(8,128)(2,1)S(1)} %get-tuple-element.9.matrix_ref, bf16[128,64,512]{2,1,0:T(8,128)(2,1)S(1)} %get-tuple-element.10.orbitals_ref), custom_call_target="tpu_custom_call" | custom-call | flops 12884901888 | bytes 8388608 | tf_op jit(solution)/shard_map/stress_sums/pallas_call | solution.py:295
  34.5 0.0 copy-done
  34.5 0.1 constant_dynamic-slice_fusion
  34.5 0.1 copy.16
  34.6 0.1 pad.6.clone
  34.7 0.0 collective-permute-done
  34.7 0.0 collective-permute-done.1
  34.7 0.0 collective-permute-done.2
  34.7 0.0 collective-permute-done.3
  34.7 0.1 add_add_fusion
  34.8 0.1 fusion.2
  34.9 0.1 fusion.1
  35.0 0.1 fusion
  35.1 0.1 copy.18
  35.2 0.1 select_maximum_fusion
  35.3 1.5 %collective-permute-start.5 = (f32[16,128]{1,0:T(8,128)S(1)}, f32[16,128]{1,0:T(8,128)S(1)}, u32[]{:S(2)}, u32[]{:S(2)}) collective-permute-start(f32[16,128]{1,0:T(8,128)S(1)} %select_maximum_fusion), channel_id=1, source_target_pairs={{0,2},{1,3},{2,0},{3,1},{4,6},{5,7},{6,4},{7,5},{8,10},{9,11},{10,... | collective-permute-start | bytes 24584 | tf_op jit(solution)/shard_map/ppermute | solution.py:24
  36.8 0.0 collective-permute-start.6
  36.8 0.5 %collective-permute-start.4 = (f32[16,128]{1,0:T(8,128)S(1)}, f32[16,128]{1,0:T(8,128)S(1)}, u32[]{:S(2)}, u32[]{:S(2)}) collective-permute-start(f32[16,128]{1,0:T(8,128)S(1)} %select_maximum_fusion), channel_id=1, source_target_pairs={{0,1},{1,2},{2,3},{3,0},{4,5},{5,6},{6,7},{7,4},{8,9},{9,10},{10,1... | collective-permute-start | bytes 24584 | tf_op jit(solution)/shard_map/ppermute | solution.py:24
  37.3 1.7 %collective-permute-done.5 = f32[16,128]{1,0:T(8,128)S(1)} collective-permute-done((f32[16,128]{1,0:T(8,128)S(1)}, f32[16,128]{1,0:T(8,128)S(1)}, u32[]{:S(2)}, u32[]{:S(2)}) %collective-permute-start.5) | collective-permute-done | bytes 8224 | tf_op jit(solution)/shard_map/ppermute | solution.py:24
  39.0 0.0 collective-permute-done.6
  39.0 0.9 %collective-permute-done.4 = f32[16,128]{1,0:T(8,128)S(1)} collective-permute-done((f32[16,128]{1,0:T(8,128)S(1)}, f32[16,128]{1,0:T(8,128)S(1)}, u32[]{:S(2)}, u32[]{:S(2)}) %collective-permute-start.4) | collective-permute-done | bytes 8224 | tf_op jit(solution)/shard_map/ppermute | solution.py:24
  39.9 0.1 add_add_fusion.1
  39.9 0.6 %slice.29 = f32[3,8]{1,0:T(4,128)} slice(f32[16,128]{1,0:T(8,128)S(1)} %add_add_fusion.1), slice={[8:11], [0:8]} | slice | bytes 192 | tf_op jit(solution)/shard_map/slice | solution.py:373
  40.5 0.6 %slice.28 = f32[6,128]{1,0:T(8,128)} slice(f32[16,128]{1,0:T(8,128)S(1)} %add_add_fusion.1), slice={[0:6], [0:128]} | slice | bytes 6144 | tf_op jit(solution)/shard_map/slice | solution.py:373
  (3 shorter events, 0.0 us)
Async XLA Ops:
  0.6 33.8 %copy-start = (f32[64,16]{0,1:T(8,128)S(1)}, f32[64,16]{0,1:T(8,128)}, u32[]{:S(2)}) copy-start(f32[64,16]{0,1:T(8,128)} %param.17) | copy-start | bytes 12292
  0.6 16.6 %copy-start.1 = (f32[64]{0:T(128)S(1)}, f32[64]{0:T(128)}, u32[]{:S(2)}) copy-start(f32[64]{0:T(128)} %param.13) | copy-start | bytes 772
  0.7 16.6 %copy-start.2 = (f32[512]{0:T(512)S(1)}, f32[512]{0:T(512)}, u32[]{:S(2)}) copy-start(f32[512]{0:T(512)} %param.11) | copy-start | bytes 6148
  0.7 16.6 %copy-start.3 = (f32[128]{0:T(128)S(1)}, f32[128]{0:T(128)}, u32[]{:S(2)}) copy-start(f32[128]{0:T(128)} %scale_hbm.1) | copy-start | bytes 1540
  9.2 25.5 %collective-permute-start = (f32[8,32,128]{2,1,0:T(8,128)S(1)}, f32[8,32,128]{2,1,0:T(8,128)S(1)}, u32[]{:S(2)}, u32[]{:S(2)}) collective-permute-start(f32[8,32,128]{2,1,0:T(8,128)S(1)} %get-tuple-element.12), channel_id=1, source_target_pairs={{0,24},{4,28},{8,0},{12,4},{16,8},{20,12},{24,16},{28,20},{1,25},{... | collective-permute-start | bytes 393224 | tf_op jit(solution)/shard_map/ppermute | solution.py:24
  14.3 20.4 %collective-permute-start.1 = (f32[8,32,128]{2,1,0:T(8,128)S(1)}, f32[8,32,128]{2,1,0:T(8,128)S(1)}, u32[]{:S(2)}, u32[]{:S(2)}) collective-permute-start(f32[8,32,128]{2,1,0:T(8,128)S(1)} %get-tuple-element.13), channel_id=1, source_target_pairs={{0,28},{4,0},{8,4},{12,8},{16,12},{20,16},{24,20},{28,24},{1,29},{... | collective-permute-start | bytes 393224 | tf_op jit(solution)/shard_map/ppermute | solution.py:24
  15.7 19.0 %collective-permute-start.2 = (f32[8,32,128]{2,1,0:T(8,128)S(1)}, f32[8,32,128]{2,1,0:T(8,128)S(1)}, u32[]{:S(2)}, u32[]{:S(2)}) collective-permute-start(f32[8,32,128]{2,1,0:T(8,128)S(1)} %get-tuple-element.14), channel_id=1, source_target_pairs={{0,4},{4,8},{8,12},{12,16},{16,20},{20,24},{24,28},{28,0},{1,5},{5... | collective-permute-start | bytes 393224 | tf_op jit(solution)/shard_map/ppermute | solution.py:24
  16.3 18.4 %collective-permute-start.3 = (f32[8,32,128]{2,1,0:T(8,128)S(1)}, f32[8,32,128]{2,1,0:T(8,128)S(1)}, u32[]{:S(2)}, u32[]{:S(2)}) collective-permute-start(f32[8,32,128]{2,1,0:T(8,128)S(1)} %get-tuple-element.15), channel_id=1, source_target_pairs={{0,8},{4,12},{8,16},{12,20},{16,24},{20,28},{24,0},{28,4},{1,9},{5... | collective-permute-start | bytes 393224 | tf_op jit(solution)/shard_map/ppermute | solution.py:24
  35.3 3.7 %collective-permute-start.5 = (f32[16,128]{1,0:T(8,128)S(1)}, f32[16,128]{1,0:T(8,128)S(1)}, u32[]{:S(2)}, u32[]{:S(2)}) collective-permute-start(f32[16,128]{1,0:T(8,128)S(1)} %select_maximum_fusion), channel_id=1, source_target_pairs={{0,2},{1,3},{2,0},{3,1},{4,6},{5,7},{6,4},{7,5},{8,10},{9,11},{10,... | collective-permute-start | bytes 24584 | tf_op jit(solution)/shard_map/ppermute | solution.py:24
  36.8 2.2 %collective-permute-start.6 = (f32[16,128]{1,0:T(8,128)S(1)}, f32[16,128]{1,0:T(8,128)S(1)}, u32[]{:S(2)}, u32[]{:S(2)}) collective-permute-start(f32[16,128]{1,0:T(8,128)S(1)} %select_maximum_fusion), channel_id=1, source_target_pairs={{0,3},{1,0},{2,1},{3,2},{4,7},{5,4},{6,5},{7,6},{8,11},{9,8},{10,9... | collective-permute-start | bytes 24584 | tf_op jit(solution)/shard_map/ppermute | solution.py:24
  36.8 3.1 %collective-permute-start.4 = (f32[16,128]{1,0:T(8,128)S(1)}, f32[16,128]{1,0:T(8,128)S(1)}, u32[]{:S(2)}, u32[]{:S(2)}) collective-permute-start(f32[16,128]{1,0:T(8,128)S(1)} %select_maximum_fusion), channel_id=1, source_target_pairs={{0,1},{1,2},{2,3},{3,0},{4,5},{5,6},{6,7},{7,4},{8,9},{9,10},{10,1... | collective-permute-start | bytes 24584 | tf_op jit(solution)/shard_map/ppermute | solution.py:24

commit v3 on v2

--- a/solution.py
+++ b/solution.py
@@ -317,6 +317,73 @@
     )
 
 
+def combine_kernel(*refs, windows):
+    parts = refs[:windows]
+    coupling_ref, occ_ref, stress_ref, out_ref = refs[windows:]
+    atoms, high, _ = parts[0].shape
+    orbs = occ_ref.shape[1]
+    projs = coupling_ref.shape[1]
+    components = high * LANES // orbs // projs - 1
+    slab = lax.axis_index("cells")
+    share = coupling_ref[pl.ds(pl.multiple_of(slab * atoms, atoms), atoms), :]
+    down = jnp.transpose(share)
+    rows = [[] for _ in range(components)]
+    for atom in range(atoms):
+        total = parts[0][atom]
+        for part in parts[1:]:
+            total = total + part[atom]
+        whole = jnp.concatenate(
+            [total[:, k * orbs : (k + 1) * orbs] for k in range(LANES // orbs)], axis=0
+        )
+        margin = whole[:projs] * (down[:, atom : atom + 1] * occ_ref[...])
+        for i in range(components):
+            deriv = whole[(i + 1) * projs : (i + 2) * projs]
+            rows[i].append(jnp.sum(margin * deriv, axis=0, keepdims=True))
+    lane = lax.broadcasted_iota(jnp.int32, (atoms, LANES), 1)
+    line = lax.broadcasted_iota(jnp.int32, (atoms, LANES), 0)
+    out_ref[...] = jnp.zeros_like(out_ref)
+    out_ref[: stress_ref.shape[0], :] = stress_ref[...]
+    for i in range(components):
+        force = -2.0 * jnp.sum(jnp.concatenate(rows[i], axis=0), axis=1, keepdims=True)
+        out_ref[SUBLANES + i : SUBLANES + i + 1, :LANES] = jnp.sum(
+            jnp.where(lane == line, force, 0.0), axis=0, keepdims=True
+        )
+
+
+def combine(parts, proj_coupling, occupations, stress_part, slab_total):
+    return pl.pallas_call(
+        functools.partial(combine_kernel, windows=len(parts)),
+        out_shape=jax.ShapeDtypeStruct((2 * SUBLANES, stress_part.shape[1]), jnp.float32),
+        in_specs=[VMEM] * (len(parts) + 3),
+        out_specs=VMEM,
+        compiler_params=pltpu.CompilerParams(vmem_limit_bytes=8 << 20),
+        name="combine",
+    )(*parts, proj_coupling, occupations.reshape(1, -1), stress_part)
+
+
+def add_kernel(*refs):
+    stress_ref, force_ref = refs[-2:]
+    total = refs[0][...]
+    for ref in refs[1:-2]:
+        total = total + ref[...]
+    stress_ref[...] = total[: stress_ref.shape[0]]
+    force_ref[...] = total[SUBLANES : SUBLANES + force_ref.shape[0], : force_ref.shape[1]]
+
+
+def add_up(copies, atoms):
+    return pl.pallas_call(
+        add_kernel,
+        out_shape=(
+            jax.ShapeDtypeStruct((len(PAIRS), copies[0].shape[1]), jnp.float32),
+            jax.ShapeDtypeStruct((3, atoms), jnp.float32),
+        ),
+        in_specs=[VMEM] * len(copies),
+        out_specs=(VMEM, VMEM),
+        compiler_params=pltpu.CompilerParams(vmem_limit_bytes=8 << 20),
+        name="add_up",
+    )(*copies)
+
+
 def local(
     orbitals,
     gradient_matrix,
@@ -329,11 +396,9 @@
     proj_coupling,
 ):
     cells, orbital_count, node_count = orbitals.shape
-    proj_count = proj_values.shape[1]
     atom_total = proj_coupling.shape[0]
     slab_total = lax.axis_size("cells")
     atom_share = atom_total // slab_total
-    slab_index = lax.axis_index("cells")
     orbital_total = orbital_count * lax.axis_size("orb")
 
     parts, near_matrix, near_orbitals = window_sums(
@@ -347,30 +412,22 @@
         atom_share,
         slab_total,
     )
-    owned = parts[REACH]
-    for offset in range(-REACH, REACH + 1):
-        if offset != 0:
-            owned = owned + from_behind(parts[offset + REACH], "cells", offset)
+    received = [
+        from_behind(parts[offset + REACH], "cells", offset) for offset in (2, 1, -1, -2)
+    ]
 
     stress_part = stress_sums(
         occupations, quad_weights, cell_scale, near_matrix, near_orbitals, orbital_total
     )
 
-    fold_by = LANES // orbital_count
-    owned = jnp.concatenate(
-        [owned[:, :, k * orbital_count : (k + 1) * orbital_count] for k in range(fold_by)], axis=1
-    )
-    owned = owned.reshape(atom_share, 4, proj_count, orbital_count)
-    coupling = lax.dynamic_slice_in_dim(proj_coupling, slab_index * atom_share, atom_share, 0)
-    weight_terms = coupling[:, :, None] * occupations[None, None, :]
-    force_part = -2.0 * jnp.sum(owned[:, 1:] * (owned[:, 0] * weight_terms)[:, None], axis=(2, 3))
-    force_part = jnp.pad(
-        jnp.transpose(force_part), ((0, SUBLANES - 3), (0, cells - atom_share))
-    )
-    packed = jnp.concatenate([stress_part, jnp.zeros((2, cells), jnp.float32), force_part], axis=0)
-    copies = [packed] + [from_behind(packed, "orb", by) for by in range(1, lax.axis_size("orb"))]
-    total = functools.reduce(jnp.add, copies)
-    return (total[:6], total[8:11, :atom_share])
+    packed = combine(
+        [parts[REACH]] + received, proj_coupling, occupations, stress_part, slab_total
+    )
+    size = lax.axis_size("orb")
+    copies = [packed] + [
+        lax.ppermute(packed, "orb", [(i, i ^ by) for i in range(size)]) for by in range(size - 1, 0, -1)
+    ]
+    return add_up(copies, atom_share)
 
 
 def solution(mesh):

time: 41.3 us -> 39.5 us (0.956)
  local copies, waits for them, and re-layouts: 1.59 us -> 0.1 us
  Pallas kernels: 25.6 us -> 26.5 us
  waiting for transfers between devices: 2.58 us -> 1.9 us
  other arithmetic: 0.45 us -> 0 us
    ppermute x7 -> x4, waiting for transfers between devices: 2.58 us -> 0.01 us  [from_behind(): lax.ppermute(shard, axis, [(i, (i + by) % length) for i in range(length)])]
    ppermute x7 -> x4, starting transfers between devices: 10.1 us -> 8.11 us  [from_behind(): lax.ppermute(shard, axis, [(i, (i + by) % length) for i in range(length)])]
    ppermute x0 -> x3, starting transfers between devices: none -> 1.93 us  [local(): lax.ppermute(packed, 'orb', [(i, i ^ by) for i in range(size)])]
    ppermute x0 -> x3, waiting for transfers between devices: none -> 1.89 us  [local(): lax.ppermute(packed, 'orb', [(i, i ^ by) for i in range(size)])]
    slice x3 -> x0, local copies, waits for them, and re-layouts: 1.27 us -> none  [the longest x2 1.18 us: local(): return (total[:6], total[8:11, :atom_share])]
    pallas_call x0 -> x2, Pallas kernels: none -> 0.9 us  [the longest x1 0.6 us: add_up(): pl.pallas_call(add_kernel, out_shape=(jax.ShapeDtypeStruct((len(PAIRS), c...]
  transfers between devices with their start and end apart: 7 -> 7, of which waited for: 2 -> 2; matrix products, arithmetic and copies ran while one was open for 1% -> 0% of each run, Pallas kernels for 42% -> 44%
where the time goes in v3:
time: 39.5 us; the launch traced here: 39.3 us
  Pallas kernels  26.5 us (67%)
  starting transfers between devices  10 us (25%)
  waiting for transfers between devices  1.9 us (5%)
  between operations  0.72 us (2%)
    pallas_call x1, Pallas kernels, stress_sums(): pl.pallas_call(functools.partial(stress_kernel, share=1.0 / orbital_total...  17.2 us
    pallas_call x1, Pallas kernels, window_sums(): pl.pallas_call(functools.partial(force_kernel, window_slabs=window_slabs,...  8.46 us
    ppermute x4, starting transfers between devices, from_behind(): lax.ppermute(shard, axis, [(i, (i + by) % length) for i in range(length)])  8.11 us
    ppermute x3, starting transfers between devices, local(): lax.ppermute(packed, 'orb', [(i, i ^ by) for i in range(size)])  1.93 us
    ppermute x3, waiting for transfers between devices, local(): lax.ppermute(packed, 'orb', [(i, i ^ by) for i in range(size)])  1.89 us
  transfers between devices with their start and end apart: 7, of which 2 were waited for; matrix products, arithmetic and copies ran while one was open for 0% of the time, Pallas kernels for 44%

profile of v3, /device:TPU:0, one launch (start us, length us, event | category | flops | bytes accessed | tf_op | source)
XLA Modules:
  0.0 39.3 jit_solution(7589147306819443887)
XLA Ops:
  0.6 0.0 copy-start
  0.6 0.0 copy-start.1
  0.7 0.0 copy-start.2
  0.7 8.5 %window_sums.1 = (f32[8,32,128]{2,1,0:T(8,128)S(1)}, f32[8,32,128]{2,1,0:T(8,128)S(1)}, f32[8,32,128]{2,1,0:T(8,128)S(1)}, f32[8,32,128]{2,1,0:T(8,128)S(1)}, f3...) custom-call(s32[128]{0:T(128)} %cell_hbm.1, s32[128]{0:T(128)} %atom_hbm.1, ...), custom_call_target="tpu_custom_call" | custom-call | flops 3758096384 | bytes 10485760 | tf_op jit(solution)/shard_map/window_sums/pallas_call | solution.py:156
  9.1 3.1 %collective-permute-start = (f32[8,32,128]{2,1,0:T(8,128)S(1)}, f32[8,32,128]{2,1,0:T(8,128)S(1)}, u32[]{:S(2)}, u32[]{:S(2)}) collective-permute-start(f32[8,32,128]{2,1,0:T(8,128)S(1)} %get-tuple-element.10), channel_id=1, source_target_pairs={{0,8},{4,12},{8,16},{12,20},{16,24},{20,28},{24,0},{28,4},{1,9},{5... | collective-permute-start | bytes 393224 | tf_op jit(solution)/shard_map/ppermute | solution.py:24
  12.2 1.5 %collective-permute-start.1 = (f32[8,32,128]{2,1,0:T(8,128)S(1)}, f32[8,32,128]{2,1,0:T(8,128)S(1)}, u32[]{:S(2)}, u32[]{:S(2)}) collective-permute-start(f32[8,32,128]{2,1,0:T(8,128)S(1)} %get-tuple-element.11), channel_id=1, source_target_pairs={{0,4},{4,8},{8,12},{12,16},{16,20},{20,24},{24,28},{28,0},{1,5},{5... | collective-permute-start | bytes 393224 | tf_op jit(solution)/shard_map/ppermute | solution.py:24
  13.7 3.2 %collective-permute-start.2 = (f32[8,32,128]{2,1,0:T(8,128)S(1)}, f32[8,32,128]{2,1,0:T(8,128)S(1)}, u32[]{:S(2)}, u32[]{:S(2)}) collective-permute-start(f32[8,32,128]{2,1,0:T(8,128)S(1)} %get-tuple-element.12), channel_id=1, source_target_pairs={{0,28},{4,0},{8,4},{12,8},{16,12},{20,16},{24,20},{28,24},{1,29},{... | collective-permute-start | bytes 393224 | tf_op jit(solution)/shard_map/ppermute | solution.py:24
  17.0 0.3 collective-permute-start.3
  17.2 0.0 copy-done
  17.2 0.0 copy-done.1
  17.2 0.0 copy-done.2
  17.2 0.0 copy-start.3
  17.3 17.2 %stress_sums.1.refs_7_ = f32[6,128]{1,0:T(8,128)S(1)} custom-call(f32[1,64]{1,0:T(1,128)S(1)} %bitcast.3, f32[1,512]{1,0:T(1,128)S(1)} %bitcast.6, f32[1,128]{1,0:T(1,128)S(1)} %bitcast.7, bf16[512,1536]{1,0:T(8,128)(2,1)S(1)} %get-tuple-element.14.matrix_ref, bf16[128,64,512]{2,1,0:T(8,128)(2,1)S(1)} %get-tuple-element.15.orbitals_ref), custom_call_target="tpu_custom_call" | custom-call | flops 12884901888 | bytes 8388608 | tf_op jit(solution)/shard_map/stress_sums/pallas_call | solution.py:295
  34.4 0.0 copy-done.3
  34.4 0.1 copy.11.refs_5_
  34.5 0.0 collective-permute-done.refs_1_
  34.5 0.0 collective-permute-done.1.refs_2_
  34.5 0.0 collective-permute-done.2.refs_3_
  34.5 0.0 collective-permute-done.3.refs_4_
  34.5 0.3 combine.1.refs_0_
  34.8 0.2 collective-permute-start.4
  35.0 1.7 %collective-permute-start.5 = (f32[16,128]{1,0:T(8,128)S(1)}, f32[16,128]{1,0:T(8,128)S(1)}, u32[]{:S(2)}, u32[]{:S(2)}) collective-permute-start(f32[16,128]{1,0:T(8,128)S(1)} %combine.1.refs_0_), channel_id=1, source_target_pairs={{0,2},{1,3},{2,0},{3,1},{4,6},{5,7},{6,4},{7,5},{8,10},{9,11},{10,... | collective-permute-start | bytes 24584 | tf_op jit(solution)/shard_map/ppermute | solution.py:428
  36.7 0.1 collective-permute-start.6
  36.8 1.2 %collective-permute-done.4.refs_1_ = f32[16,128]{1,0:T(8,128)S(1)} collective-permute-done((f32[16,128]{1,0:T(8,128)S(1)}, f32[16,128]{1,0:T(8,128)S(1)}, u32[]{:S(2)}, u32[]{:S(2)}) %collective-permute-start.4) | collective-permute-done | bytes 8224 | tf_op jit(solution)/shard_map/ppermute | solution.py:428
  38.0 0.7 %collective-permute-done.5.refs_2_ = f32[16,128]{1,0:T(8,128)S(1)} collective-permute-done((f32[16,128]{1,0:T(8,128)S(1)}, f32[16,128]{1,0:T(8,128)S(1)}, u32[]{:S(2)}, u32[]{:S(2)}) %collective-permute-start.5) | collective-permute-done | bytes 8224 | tf_op jit(solution)/shard_map/ppermute | solution.py:428
  38.7 0.0 collective-permute-done.6.refs_3_
  38.7 0.6 %add_up.1 = (f32[6,128]{1,0:T(8,128)}, f32[3,8]{1,0:T(4,128)}) custom-call(f32[16,128]{1,0:T(8,128)S(1)} %combine.1.refs_0_, f32[16,128]{1,0:T(8,128)S(1)} %collective-permute-done.4.refs_1_, f32[16,128]{1,0:T(8,128)S(1)} %collective-permute-done.5.refs_2_, f32[16,128]{1,0:T(8,128)S(1)} %collective-permute-done.6.refs_3_), custom_call_target="tpu_custom_call" | custom-call | tf_op jit(solution)/shard_map/add_up/pallas_call | solution.py:374
Async XLA Ops:
  0.6 16.6 %copy-start = (f32[64]{0:T(128)S(1)}, f32[64]{0:T(128)}, u32[]{:S(2)}) copy-start(f32[64]{0:T(128)} %param.13) | copy-start | bytes 772
  0.6 16.6 %copy-start.1 = (f32[512]{0:T(512)S(1)}, f32[512]{0:T(512)}, u32[]{:S(2)}) copy-start(f32[512]{0:T(512)} %param.11) | copy-start | bytes 6148
  0.7 16.6 %copy-start.2 = (f32[128]{0:T(128)S(1)}, f32[128]{0:T(128)}, u32[]{:S(2)}) copy-start(f32[128]{0:T(128)} %scale_hbm.1) | copy-start | bytes 1540
  9.1 25.4 %collective-permute-start = (f32[8,32,128]{2,1,0:T(8,128)S(1)}, f32[8,32,128]{2,1,0:T(8,128)S(1)}, u32[]{:S(2)}, u32[]{:S(2)}) collective-permute-start(f32[8,32,128]{2,1,0:T(8,128)S(1)} %get-tuple-element.10), channel_id=1, source_target_pairs={{0,8},{4,12},{8,16},{12,20},{16,24},{20,28},{24,0},{28,4},{1,9},{5... | collective-permute-start | bytes 393224 | tf_op jit(solution)/shard_map/ppermute | solution.py:24
  12.2 22.3 %collective-permute-start.1 = (f32[8,32,128]{2,1,0:T(8,128)S(1)}, f32[8,32,128]{2,1,0:T(8,128)S(1)}, u32[]{:S(2)}, u32[]{:S(2)}) collective-permute-start(f32[8,32,128]{2,1,0:T(8,128)S(1)} %get-tuple-element.11), channel_id=1, source_target_pairs={{0,4},{4,8},{8,12},{12,16},{16,20},{20,24},{24,28},{28,0},{1,5},{5... | collective-permute-start | bytes 393224 | tf_op jit(solution)/shard_map/ppermute | solution.py:24
  13.7 20.8 %collective-permute-start.2 = (f32[8,32,128]{2,1,0:T(8,128)S(1)}, f32[8,32,128]{2,1,0:T(8,128)S(1)}, u32[]{:S(2)}, u32[]{:S(2)}) collective-permute-start(f32[8,32,128]{2,1,0:T(8,128)S(1)} %get-tuple-element.12), channel_id=1, source_target_pairs={{0,28},{4,0},{8,4},{12,8},{16,12},{20,16},{24,20},{28,24},{1,29},{... | collective-permute-start | bytes 393224 | tf_op jit(solution)/shard_map/ppermute | solution.py:24
  17.0 17.6 %collective-permute-start.3 = (f32[8,32,128]{2,1,0:T(8,128)S(1)}, f32[8,32,128]{2,1,0:T(8,128)S(1)}, u32[]{:S(2)}, u32[]{:S(2)}) collective-permute-start(f32[8,32,128]{2,1,0:T(8,128)S(1)} %get-tuple-element.13), channel_id=1, source_target_pairs={{0,24},{4,28},{8,0},{12,4},{16,8},{20,12},{24,16},{28,20},{1,25},{... | collective-permute-start | bytes 393224 | tf_op jit(solution)/shard_map/ppermute | solution.py:24
  17.2 17.2 %copy-start.3 = (f32[64,16]{0,1:T(8,128)S(1)}, f32[64,16]{0,1:T(8,128)}, u32[]{:S(2)}) copy-start(f32[64,16]{0,1:T(8,128)} %param.17) | copy-start | bytes 12292
  34.8 3.1 %collective-permute-start.4 = (f32[16,128]{1,0:T(8,128)S(1)}, f32[16,128]{1,0:T(8,128)S(1)}, u32[]{:S(2)}, u32[]{:S(2)}) collective-permute-start(f32[16,128]{1,0:T(8,128)S(1)} %combine.1.refs_0_), channel_id=1, source_target_pairs={{0,3},{1,2},{2,1},{3,0},{4,7},{5,6},{6,5},{7,4},{8,11},{9,10},{10,... | collective-permute-start | bytes 24584 | tf_op jit(solution)/shard_map/ppermute | solution.py:428
  35.0 3.7 %collective-permute-start.5 = (f32[16,128]{1,0:T(8,128)S(1)}, f32[16,128]{1,0:T(8,128)S(1)}, u32[]{:S(2)}, u32[]{:S(2)}) collective-permute-start(f32[16,128]{1,0:T(8,128)S(1)} %combine.1.refs_0_), channel_id=1, source_target_pairs={{0,2},{1,3},{2,0},{3,1},{4,6},{5,7},{6,4},{7,5},{8,10},{9,11},{10,... | collective-permute-start | bytes 24584 | tf_op jit(solution)/shard_map/ppermute | solution.py:428
  36.7 2.0 %collective-permute-start.6 = (f32[16,128]{1,0:T(8,128)S(1)}, f32[16,128]{1,0:T(8,128)S(1)}, u32[]{:S(2)}, u32[]{:S(2)}) collective-permute-start(f32[16,128]{1,0:T(8,128)S(1)} %combine.1.refs_0_), channel_id=1, source_target_pairs={{0,1},{1,0},{2,3},{3,2},{4,5},{5,4},{6,7},{7,6},{8,9},{9,8},{10,11... | collective-permute-start | bytes 24584 | tf_op jit(solution)/shard_map/ppermute | solution.py:428

commit v4 on v3

--- a/solution.py
+++ b/solution.py
@@ -226,11 +226,13 @@
     down = jnp.sum(jnp.where(rows == columns, across, 0.0), axis=1, keepdims=True)
     weight_ref[...] = down * quad_ref[...] * share
 
-    def gradient_part(i, buffer, part):
+    def gradient_part(i, buffer, part, first=0, last=block):
         at = slice(part * nodes, (part + 1) * nodes)
-        flat = orbitals_ref[pl.ds(pl.multiple_of(i * block, block), block)]
-        buffer[:, at] = jnp.dot(
-            flat.reshape(block * orbs, nodes), matrix_ref[:, at], preferred_element_type=jnp.float32
+        flat = orbitals_ref[pl.ds(i * block + first, last - first)]
+        buffer[first * orbs : last * orbs, at] = jnp.dot(
+            flat.reshape((last - first) * orbs, nodes),
+            matrix_ref[:, at],
+            preferred_element_type=jnp.float32,
         )
 
     def reduce_cells(buffer, first, last, totals):
@@ -274,9 +276,17 @@
         return carry
 
     lax.fori_loop(0, blocks // 2 - 1, pair, 0)
-    both(blocks - 2, even, odd)
+    middle = block // 2
+    before = [[] for _ in PAIRS]
     totals = [[] for _ in PAIRS]
-    reduce_cells(odd, 0, block, totals)
+    for part in range(3):
+        reduce_cells(even, part * block // 3, (part + 1) * block // 3, before)
+        gradient_part(blocks - 1, odd, part, 0, middle)
+    store(blocks - 2, before)
+    for part in range(3):
+        reduce_cells(odd, part * middle // 3, (part + 1) * middle // 3, totals)
+        gradient_part(blocks - 1, odd, part, middle, block)
+    reduce_cells(odd, middle, block, totals)
     store(blocks - 1, totals)
 
     whole = [jnp.sum(jnp.transpose(sums[k]), axis=0, keepdims=True) for k in range(len(PAIRS))]

time: 39.5 us -> 39.2 us (level)
  transfers between devices with their start and end apart: 7 -> 7, of which waited for: 2 -> 2; matrix products, arithmetic and copies ran while one was open for 0% -> 0% of each run, Pallas kernels for 44% -> 43%
where the time goes in v4:
time: 39.2 us; the launch traced here: 39 us
  Pallas kernels  26.2 us (67%)
  starting transfers between devices  10.1 us (26%)
  waiting for transfers between devices  1.88 us (5%)
  between operations  0.72 us (2%)
    pallas_call x1, Pallas kernels, stress_sums(): pl.pallas_call(functools.partial(stress_kernel, share=1.0 / orbital_total...  16.9 us
    pallas_call x1, Pallas kernels, window_sums(): pl.pallas_call(functools.partial(force_kernel, window_slabs=window_slabs,...  8.45 us
    ppermute x4, starting transfers between devices, from_behind(): lax.ppermute(shard, axis, [(i, (i + by) % length) for i in range(length)])  8.13 us
    ppermute x3, starting transfers between devices, local(): lax.ppermute(packed, 'orb', [(i, i ^ by) for i in range(size)])  1.93 us
    ppermute x3, waiting for transfers between devices, local(): lax.ppermute(packed, 'orb', [(i, i ^ by) for i in range(size)])  1.87 us
  transfers between devices with their start and end apart: 7, of which 2 were waited for; matrix products, arithmetic and copies ran while one was open for 0% of the time, Pallas kernels for 43%

profile of v4, /device:TPU:0, one launch (start us, length us, event | category | flops | bytes accessed | tf_op | source)
XLA Modules:
  0.0 39.0 jit_solution(12258980477721202431)
XLA Ops:
  0.6 0.0 copy-start
  0.6 0.0 copy-start.1
  0.7 0.0 copy-start.2
  0.7 8.5 %window_sums.1 = (f32[8,32,128]{2,1,0:T(8,128)S(1)}, f32[8,32,128]{2,1,0:T(8,128)S(1)}, f32[8,32,128]{2,1,0:T(8,128)S(1)}, f32[8,32,128]{2,1,0:T(8,128)S(1)}, f3...) custom-call(s32[128]{0:T(128)} %cell_hbm.1, s32[128]{0:T(128)} %atom_hbm.1, ...), custom_call_target="tpu_custom_call" | custom-call | flops 3758096384 | bytes 10485760 | tf_op jit(solution)/shard_map/window_sums/pallas_call | solution.py:156
  9.1 3.1 %collective-permute-start = (f32[8,32,128]{2,1,0:T(8,128)S(1)}, f32[8,32,128]{2,1,0:T(8,128)S(1)}, u32[]{:S(2)}, u32[]{:S(2)}) collective-permute-start(f32[8,32,128]{2,1,0:T(8,128)S(1)} %get-tuple-element.10), channel_id=1, source_target_pairs={{0,8},{4,12},{8,16},{12,20},{16,24},{20,28},{24,0},{28,4},{1,9},{5... | collective-permute-start | bytes 393224 | tf_op jit(solution)/shard_map/ppermute | solution.py:24
  12.2 1.5 %collective-permute-start.1 = (f32[8,32,128]{2,1,0:T(8,128)S(1)}, f32[8,32,128]{2,1,0:T(8,128)S(1)}, u32[]{:S(2)}, u32[]{:S(2)}) collective-permute-start(f32[8,32,128]{2,1,0:T(8,128)S(1)} %get-tuple-element.11), channel_id=1, source_target_pairs={{0,4},{4,8},{8,12},{12,16},{16,20},{20,24},{24,28},{28,0},{1,5},{5... | collective-permute-start | bytes 393224 | tf_op jit(solution)/shard_map/ppermute | solution.py:24
  13.8 3.2 %collective-permute-start.2 = (f32[8,32,128]{2,1,0:T(8,128)S(1)}, f32[8,32,128]{2,1,0:T(8,128)S(1)}, u32[]{:S(2)}, u32[]{:S(2)}) collective-permute-start(f32[8,32,128]{2,1,0:T(8,128)S(1)} %get-tuple-element.12), channel_id=1, source_target_pairs={{0,28},{4,0},{8,4},{12,8},{16,12},{20,16},{24,20},{28,24},{1,29},{... | collective-permute-start | bytes 393224 | tf_op jit(solution)/shard_map/ppermute | solution.py:24
  17.0 0.3 collective-permute-start.3
  17.3 0.0 copy-done
  17.3 0.0 copy-done.1
  17.3 0.0 copy-done.2
  17.3 0.0 copy-start.3
  17.3 16.9 %stress_sums.1.refs_7_ = f32[6,128]{1,0:T(8,128)S(1)} custom-call(f32[1,64]{1,0:T(1,128)S(1)} %bitcast.3, f32[1,512]{1,0:T(1,128)S(1)} %bitcast.6, f32[1,128]{1,0:T(1,128)S(1)} %bitcast.7, bf16[512,1536]{1,0:T(8,128)(2,1)S(1)} %get-tuple-element.14.matrix_ref, bf16[128,64,512]{2,1,0:T(8,128)(2,1)S(1)} %get-tuple-element.15.orbitals_ref), custom_call_target="tpu_custom_call" | custom-call | flops 12884901888 | bytes 8388608 | tf_op jit(solution)/shard_map/stress_sums/pallas_call | solution.py:305
  34.1 0.0 copy-done.3
  34.1 0.1 copy.11.refs_5_
  34.2 0.0 collective-permute-done.refs_1_
  34.2 0.0 collective-permute-done.1.refs_2_
  34.2 0.0 collective-permute-done.2.refs_3_
  34.2 0.0 collective-permute-done.3.refs_4_
  34.3 0.3 combine.1.refs_0_
  34.6 0.1 collective-permute-start.4
  34.7 1.7 %collective-permute-start.5 = (f32[16,128]{1,0:T(8,128)S(1)}, f32[16,128]{1,0:T(8,128)S(1)}, u32[]{:S(2)}, u32[]{:S(2)}) collective-permute-start(f32[16,128]{1,0:T(8,128)S(1)} %combine.1.refs_0_), channel_id=1, source_target_pairs={{0,2},{1,3},{2,0},{3,1},{4,6},{5,7},{6,4},{7,5},{8,10},{9,11},{10,... | collective-permute-start | bytes 24584 | tf_op jit(solution)/shard_map/ppermute | solution.py:438
  36.4 0.1 collective-permute-start.6
  36.5 1.2 %collective-permute-done.4.refs_1_ = f32[16,128]{1,0:T(8,128)S(1)} collective-permute-done((f32[16,128]{1,0:T(8,128)S(1)}, f32[16,128]{1,0:T(8,128)S(1)}, u32[]{:S(2)}, u32[]{:S(2)}) %collective-permute-start.4) | collective-permute-done | bytes 8224 | tf_op jit(solution)/shard_map/ppermute | solution.py:438
  37.7 0.7 %collective-permute-done.5.refs_2_ = f32[16,128]{1,0:T(8,128)S(1)} collective-permute-done((f32[16,128]{1,0:T(8,128)S(1)}, f32[16,128]{1,0:T(8,128)S(1)}, u32[]{:S(2)}, u32[]{:S(2)}) %collective-permute-start.5) | collective-permute-done | bytes 8224 | tf_op jit(solution)/shard_map/ppermute | solution.py:438
  38.4 0.0 collective-permute-done.6.refs_3_
  38.4 0.6 %add_up.1 = (f32[6,128]{1,0:T(8,128)}, f32[3,8]{1,0:T(4,128)}) custom-call(f32[16,128]{1,0:T(8,128)S(1)} %combine.1.refs_0_, f32[16,128]{1,0:T(8,128)S(1)} %collective-permute-done.4.refs_1_, f32[16,128]{1,0:T(8,128)S(1)} %collective-permute-done.5.refs_2_, f32[16,128]{1,0:T(8,128)S(1)} %collective-permute-done.6.refs_3_), custom_call_target="tpu_custom_call" | custom-call | tf_op jit(solution)/shard_map/add_up/pallas_call | solution.py:384
Async XLA Ops:
  0.6 16.6 %copy-start = (f32[64]{0:T(128)S(1)}, f32[64]{0:T(128)}, u32[]{:S(2)}) copy-start(f32[64]{0:T(128)} %param.13) | copy-start | bytes 772
  0.6 16.6 %copy-start.1 = (f32[512]{0:T(512)S(1)}, f32[512]{0:T(512)}, u32[]{:S(2)}) copy-start(f32[512]{0:T(512)} %param.11) | copy-start | bytes 6148
  0.7 16.6 %copy-start.2 = (f32[128]{0:T(128)S(1)}, f32[128]{0:T(128)}, u32[]{:S(2)}) copy-start(f32[128]{0:T(128)} %scale_hbm.1) | copy-start | bytes 1540
  9.1 25.1 %collective-permute-start = (f32[8,32,128]{2,1,0:T(8,128)S(1)}, f32[8,32,128]{2,1,0:T(8,128)S(1)}, u32[]{:S(2)}, u32[]{:S(2)}) collective-permute-start(f32[8,32,128]{2,1,0:T(8,128)S(1)} %get-tuple-element.10), channel_id=1, source_target_pairs={{0,8},{4,12},{8,16},{12,20},{16,24},{20,28},{24,0},{28,4},{1,9},{5... | collective-permute-start | bytes 393224 | tf_op jit(solution)/shard_map/ppermute | solution.py:24
  12.2 22.0 %collective-permute-start.1 = (f32[8,32,128]{2,1,0:T(8,128)S(1)}, f32[8,32,128]{2,1,0:T(8,128)S(1)}, u32[]{:S(2)}, u32[]{:S(2)}) collective-permute-start(f32[8,32,128]{2,1,0:T(8,128)S(1)} %get-tuple-element.11), channel_id=1, source_target_pairs={{0,4},{4,8},{8,12},{12,16},{16,20},{20,24},{24,28},{28,0},{1,5},{5... | collective-permute-start | bytes 393224 | tf_op jit(solution)/shard_map/ppermute | solution.py:24
  13.8 20.5 %collective-permute-start.2 = (f32[8,32,128]{2,1,0:T(8,128)S(1)}, f32[8,32,128]{2,1,0:T(8,128)S(1)}, u32[]{:S(2)}, u32[]{:S(2)}) collective-permute-start(f32[8,32,128]{2,1,0:T(8,128)S(1)} %get-tuple-element.12), channel_id=1, source_target_pairs={{0,28},{4,0},{8,4},{12,8},{16,12},{20,16},{24,20},{28,24},{1,29},{... | collective-permute-start | bytes 393224 | tf_op jit(solution)/shard_map/ppermute | solution.py:24
  17.0 17.3 %collective-permute-start.3 = (f32[8,32,128]{2,1,0:T(8,128)S(1)}, f32[8,32,128]{2,1,0:T(8,128)S(1)}, u32[]{:S(2)}, u32[]{:S(2)}) collective-permute-start(f32[8,32,128]{2,1,0:T(8,128)S(1)} %get-tuple-element.13), channel_id=1, source_target_pairs={{0,24},{4,28},{8,0},{12,4},{16,8},{20,12},{24,16},{28,20},{1,25},{... | collective-permute-start | bytes 393224 | tf_op jit(solution)/shard_map/ppermute | solution.py:24
  17.3 16.9 %copy-start.3 = (f32[64,16]{0,1:T(8,128)S(1)}, f32[64,16]{0,1:T(8,128)}, u32[]{:S(2)}) copy-start(f32[64,16]{0,1:T(8,128)} %param.17) | copy-start | bytes 12292
  34.6 3.1 %collective-permute-start.4 = (f32[16,128]{1,0:T(8,128)S(1)}, f32[16,128]{1,0:T(8,128)S(1)}, u32[]{:S(2)}, u32[]{:S(2)}) collective-permute-start(f32[16,128]{1,0:T(8,128)S(1)} %combine.1.refs_0_), channel_id=1, source_target_pairs={{0,3},{1,2},{2,1},{3,0},{4,7},{5,6},{6,5},{7,4},{8,11},{9,10},{10,... | collective-permute-start | bytes 24584 | tf_op jit(solution)/shard_map/ppermute | solution.py:438
  34.7 3.7 %collective-permute-start.5 = (f32[16,128]{1,0:T(8,128)S(1)}, f32[16,128]{1,0:T(8,128)S(1)}, u32[]{:S(2)}, u32[]{:S(2)}) collective-permute-start(f32[16,128]{1,0:T(8,128)S(1)} %combine.1.refs_0_), channel_id=1, source_target_pairs={{0,2},{1,3},{2,0},{3,1},{4,6},{5,7},{6,4},{7,5},{8,10},{9,11},{10,... | collective-permute-start | bytes 24584 | tf_op jit(solution)/shard_map/ppermute | solution.py:438
  36.4 2.0 %collective-permute-start.6 = (f32[16,128]{1,0:T(8,128)S(1)}, f32[16,128]{1,0:T(8,128)S(1)}, u32[]{:S(2)}, u32[]{:S(2)}) collective-permute-start(f32[16,128]{1,0:T(8,128)S(1)} %combine.1.refs_0_), channel_id=1, source_target_pairs={{0,1},{1,0},{2,3},{3,2},{4,5},{5,4},{6,7},{7,6},{8,9},{9,8},{10,11... | collective-permute-start | bytes 24584 | tf_op jit(solution)/shard_map/ppermute | solution.py:438

commit v5 on v4

--- a/solution.py
+++ b/solution.py
@@ -83,6 +83,8 @@
     acc[...] = jnp.zeros_like(acc)
     load_quad.wait()
     load_proj[0].wait()
+    for load in load_matrix:
+        load.wait()
     load_orbitals.start()
 
     for c in range(chunks):
@@ -93,8 +95,6 @@
         folded[at, 0] = scaled
         flat = scaled.reshape(chunk * projs, nodes)
         for i in range(parts - 1):
-            if c == 0:
-                load_matrix[i].wait()
             part = lax.dot_general(
                 flat,
                 matrix_ref[:, i * nodes : (i + 1) * nodes],

time: 39.2 us -> 39 us (level)
  no operation moved by 1% of the time
where the time goes in v5:
time: 39 us; the launch traced here: 38.8 us
  Pallas kernels  26.1 us (67%)
  starting transfers between devices  10 us (26%)
  waiting for transfers between devices  1.89 us (5%)
  between operations  0.72 us (2%)
    pallas_call x1, Pallas kernels, stress_sums(): pl.pallas_call(functools.partial(stress_kernel, share=1.0 / orbital_total...  16.9 us
    pallas_call x1, Pallas kernels, window_sums(): pl.pallas_call(functools.partial(force_kernel, window_slabs=window_slabs,...  8.32 us
    ppermute x4, starting transfers between devices, from_behind(): lax.ppermute(shard, axis, [(i, (i + by) % length) for i in range(length)])  8.11 us
    ppermute x3, starting transfers between devices, local(): lax.ppermute(packed, 'orb', [(i, i ^ by) for i in range(size)])  1.93 us
    ppermute x3, waiting for transfers between devices, local(): lax.ppermute(packed, 'orb', [(i, i ^ by) for i in range(size)])  1.88 us
  transfers between devices with their start and end apart: 7, of which 2 were waited for; matrix products, arithmetic and copies ran while one was open for 0% of the time, Pallas kernels for 43%

profile of v5, /device:TPU:0, one launch (start us, length us, event | category | flops | bytes accessed | tf_op | source)
XLA Modules:
  0.0 38.8 jit_solution(17670744757155368750)
XLA Ops:
  0.6 0.0 copy-start
  0.6 0.0 copy-start.1
  0.7 0.0 copy-start.2
  0.7 8.3 %window_sums.1 = (f32[8,32,128]{2,1,0:T(8,128)S(1)}, f32[8,32,128]{2,1,0:T(8,128)S(1)}, f32[8,32,128]{2,1,0:T(8,128)S(1)}, f32[8,32,128]{2,1,0:T(8,128)S(1)}, f3...) custom-call(s32[128]{0:T(128)} %cell_hbm.1, s32[128]{0:T(128)} %atom_hbm.1, ...), custom_call_target="tpu_custom_call" | custom-call | flops 3758096384 | bytes 10485760 | tf_op jit(solution)/shard_map/window_sums/pallas_call | solution.py:156
  9.0 3.1 %collective-permute-start = (f32[8,32,128]{2,1,0:T(8,128)S(1)}, f32[8,32,128]{2,1,0:T(8,128)S(1)}, u32[]{:S(2)}, u32[]{:S(2)}) collective-permute-start(f32[8,32,128]{2,1,0:T(8,128)S(1)} %get-tuple-element.10), channel_id=1, source_target_pairs={{0,8},{4,12},{8,16},{12,20},{16,24},{20,28},{24,0},{28,4},{1,9},{5... | collective-permute-start | bytes 393224 | tf_op jit(solution)/shard_map/ppermute | solution.py:24
  12.1 1.5 %collective-permute-start.1 = (f32[8,32,128]{2,1,0:T(8,128)S(1)}, f32[8,32,128]{2,1,0:T(8,128)S(1)}, u32[]{:S(2)}, u32[]{:S(2)}) collective-permute-start(f32[8,32,128]{2,1,0:T(8,128)S(1)} %get-tuple-element.11), channel_id=1, source_target_pairs={{0,4},{4,8},{8,12},{12,16},{16,20},{20,24},{24,28},{28,0},{1,5},{5... | collective-permute-start | bytes 393224 | tf_op jit(solution)/shard_map/ppermute | solution.py:24
  13.6 3.2 %collective-permute-start.2 = (f32[8,32,128]{2,1,0:T(8,128)S(1)}, f32[8,32,128]{2,1,0:T(8,128)S(1)}, u32[]{:S(2)}, u32[]{:S(2)}) collective-permute-start(f32[8,32,128]{2,1,0:T(8,128)S(1)} %get-tuple-element.12), channel_id=1, source_target_pairs={{0,28},{4,0},{8,4},{12,8},{16,12},{20,16},{24,20},{28,24},{1,29},{... | collective-permute-start | bytes 393224 | tf_op jit(solution)/shard_map/ppermute | solution.py:24
  16.8 0.3 collective-permute-start.3
  17.1 0.0 copy-done
  17.1 0.0 copy-done.1
  17.1 0.0 copy-done.2
  17.1 0.0 copy-start.3
  17.1 16.9 %stress_sums.1.refs_7_ = f32[6,128]{1,0:T(8,128)S(1)} custom-call(f32[1,64]{1,0:T(1,128)S(1)} %bitcast.3, f32[1,512]{1,0:T(1,128)S(1)} %bitcast.6, f32[1,128]{1,0:T(1,128)S(1)} %bitcast.7, bf16[512,1536]{1,0:T(8,128)(2,1)S(1)} %get-tuple-element.14.matrix_ref, bf16[128,64,512]{2,1,0:T(8,128)(2,1)S(1)} %get-tuple-element.15.orbitals_ref), custom_call_target="tpu_custom_call" | custom-call | flops 12884901888 | bytes 8388608 | tf_op jit(solution)/shard_map/stress_sums/pallas_call | solution.py:305
  34.0 0.0 copy-done.3
  34.0 0.1 copy.11.refs_5_
  34.1 0.0 collective-permute-done.refs_1_
  34.1 0.0 collective-permute-done.1.refs_2_
  34.1 0.0 collective-permute-done.2.refs_3_
  34.1 0.0 collective-permute-done.3.refs_4_
  34.1 0.3 combine.1.refs_0_
  34.4 0.2 collective-permute-start.4
  34.6 1.6 %collective-permute-start.5 = (f32[16,128]{1,0:T(8,128)S(1)}, f32[16,128]{1,0:T(8,128)S(1)}, u32[]{:S(2)}, u32[]{:S(2)}) collective-permute-start(f32[16,128]{1,0:T(8,128)S(1)} %combine.1.refs_0_), channel_id=1, source_target_pairs={{0,2},{1,3},{2,0},{3,1},{4,6},{5,7},{6,4},{7,5},{8,10},{9,11},{10,... | collective-permute-start | bytes 24584 | tf_op jit(solution)/shard_map/ppermute | solution.py:438
  36.2 0.1 collective-permute-start.6
  36.4 1.2 %collective-permute-done.4.refs_1_ = f32[16,128]{1,0:T(8,128)S(1)} collective-permute-done((f32[16,128]{1,0:T(8,128)S(1)}, f32[16,128]{1,0:T(8,128)S(1)}, u32[]{:S(2)}, u32[]{:S(2)}) %collective-permute-start.4) | collective-permute-done | bytes 8224 | tf_op jit(solution)/shard_map/ppermute | solution.py:438
  37.6 0.7 %collective-permute-done.5.refs_2_ = f32[16,128]{1,0:T(8,128)S(1)} collective-permute-done((f32[16,128]{1,0:T(8,128)S(1)}, f32[16,128]{1,0:T(8,128)S(1)}, u32[]{:S(2)}, u32[]{:S(2)}) %collective-permute-start.5) | collective-permute-done | bytes 8224 | tf_op jit(solution)/shard_map/ppermute | solution.py:438
  38.2 0.0 collective-permute-done.6.refs_3_
  38.2 0.6 %add_up.1 = (f32[6,128]{1,0:T(8,128)}, f32[3,8]{1,0:T(4,128)}) custom-call(f32[16,128]{1,0:T(8,128)S(1)} %combine.1.refs_0_, f32[16,128]{1,0:T(8,128)S(1)} %collective-permute-done.4.refs_1_, f32[16,128]{1,0:T(8,128)S(1)} %collective-permute-done.5.refs_2_, f32[16,128]{1,0:T(8,128)S(1)} %collective-permute-done.6.refs_3_), custom_call_target="tpu_custom_call" | custom-call | tf_op jit(solution)/shard_map/add_up/pallas_call | solution.py:384
Async XLA Ops:
  0.6 16.5 %copy-start = (f32[64]{0:T(128)S(1)}, f32[64]{0:T(128)}, u32[]{:S(2)}) copy-start(f32[64]{0:T(128)} %param.13) | copy-start | bytes 772
  0.6 16.5 %copy-start.1 = (f32[512]{0:T(512)S(1)}, f32[512]{0:T(512)}, u32[]{:S(2)}) copy-start(f32[512]{0:T(512)} %param.11) | copy-start | bytes 6148
  0.7 16.5 %copy-start.2 = (f32[128]{0:T(128)S(1)}, f32[128]{0:T(128)}, u32[]{:S(2)}) copy-start(f32[128]{0:T(128)} %scale_hbm.1) | copy-start | bytes 1540
  9.0 25.1 %collective-permute-start = (f32[8,32,128]{2,1,0:T(8,128)S(1)}, f32[8,32,128]{2,1,0:T(8,128)S(1)}, u32[]{:S(2)}, u32[]{:S(2)}) collective-permute-start(f32[8,32,128]{2,1,0:T(8,128)S(1)} %get-tuple-element.10), channel_id=1, source_target_pairs={{0,8},{4,12},{8,16},{12,20},{16,24},{20,28},{24,0},{28,4},{1,9},{5... | collective-permute-start | bytes 393224 | tf_op jit(solution)/shard_map/ppermute | solution.py:24
  12.1 22.0 %collective-permute-start.1 = (f32[8,32,128]{2,1,0:T(8,128)S(1)}, f32[8,32,128]{2,1,0:T(8,128)S(1)}, u32[]{:S(2)}, u32[]{:S(2)}) collective-permute-start(f32[8,32,128]{2,1,0:T(8,128)S(1)} %get-tuple-element.11), channel_id=1, source_target_pairs={{0,4},{4,8},{8,12},{12,16},{16,20},{20,24},{24,28},{28,0},{1,5},{5... | collective-permute-start | bytes 393224 | tf_op jit(solution)/shard_map/ppermute | solution.py:24
  13.6 20.5 %collective-permute-start.2 = (f32[8,32,128]{2,1,0:T(8,128)S(1)}, f32[8,32,128]{2,1,0:T(8,128)S(1)}, u32[]{:S(2)}, u32[]{:S(2)}) collective-permute-start(f32[8,32,128]{2,1,0:T(8,128)S(1)} %get-tuple-element.12), channel_id=1, source_target_pairs={{0,28},{4,0},{8,4},{12,8},{16,12},{20,16},{24,20},{28,24},{1,29},{... | collective-permute-start | bytes 393224 | tf_op jit(solution)/shard_map/ppermute | solution.py:24
  16.8 17.3 %collective-permute-start.3 = (f32[8,32,128]{2,1,0:T(8,128)S(1)}, f32[8,32,128]{2,1,0:T(8,128)S(1)}, u32[]{:S(2)}, u32[]{:S(2)}) collective-permute-start(f32[8,32,128]{2,1,0:T(8,128)S(1)} %get-tuple-element.13), channel_id=1, source_target_pairs={{0,24},{4,28},{8,0},{12,4},{16,8},{20,12},{24,16},{28,20},{1,25},{... | collective-permute-start | bytes 393224 | tf_op jit(solution)/shard_map/ppermute | solution.py:24
  17.1 16.9 %copy-start.3 = (f32[64,16]{0,1:T(8,128)S(1)}, f32[64,16]{0,1:T(8,128)}, u32[]{:S(2)}) copy-start(f32[64,16]{0,1:T(8,128)} %param.17) | copy-start | bytes 12292
  34.4 3.1 %collective-permute-start.4 = (f32[16,128]{1,0:T(8,128)S(1)}, f32[16,128]{1,0:T(8,128)S(1)}, u32[]{:S(2)}, u32[]{:S(2)}) collective-permute-start(f32[16,128]{1,0:T(8,128)S(1)} %combine.1.refs_0_), channel_id=1, source_target_pairs={{0,3},{1,2},{2,1},{3,0},{4,7},{5,6},{6,5},{7,4},{8,11},{9,10},{10,... | collective-permute-start | bytes 24584 | tf_op jit(solution)/shard_map/ppermute | solution.py:438
  34.6 3.7 %collective-permute-start.5 = (f32[16,128]{1,0:T(8,128)S(1)}, f32[16,128]{1,0:T(8,128)S(1)}, u32[]{:S(2)}, u32[]{:S(2)}) collective-permute-start(f32[16,128]{1,0:T(8,128)S(1)} %combine.1.refs_0_), channel_id=1, source_target_pairs={{0,2},{1,3},{2,0},{3,1},{4,6},{5,7},{6,4},{7,5},{8,10},{9,11},{10,... | collective-permute-start | bytes 24584 | tf_op jit(solution)/shard_map/ppermute | solution.py:438
  36.2 2.0 %collective-permute-start.6 = (f32[16,128]{1,0:T(8,128)S(1)}, f32[16,128]{1,0:T(8,128)S(1)}, u32[]{:S(2)}, u32[]{:S(2)}) collective-permute-start(f32[16,128]{1,0:T(8,128)S(1)} %combine.1.refs_0_), channel_id=1, source_target_pairs={{0,1},{1,0},{2,3},{3,2},{4,5},{5,4},{6,7},{7,6},{8,9},{9,8},{10,11... | collective-permute-start | bytes 24584 | tf_op jit(solution)/shard_map/ppermute | solution.py:438
